TPU v7x, 32 devices: a whole 2x2x4 slice. The times are simulated.
32 devices in a mesh: sector: 4 (over y, x), bin: 8 (over z, core).
Axes of the slice: x: 2, y: 2, z: 4, core: 2. Of those that a mesh axis runs over, the one named last changes fastest.
Arguments:
- sph_state: float32 [7, 32768], P(None, ('sector', 'bin')), as said below
- sph_dest: int32 [32768, 1], P(('sector', 'bin')), may hold values from 0 to 31; in each aligned block of 1024 rows (0 to 1023, 1024 to 2047, ...) at most 64 rows name the same one
- body_list: int32 [32, 2], P(('sector', 'bin')), may hold values from 0 to 3, all different within a row
- tile_codes: int32 [32, 2, 32], P(('sector', 'bin')), may hold values from 0 to 511, as said below
- triangles: float32 [9, 4, 32768], P(None, 'sector', 'bin'), as said below
Outputs:
- new_state: float32 [7, 65536], P(None, ('sector', 'bin'))
- body_kick: float32 [4, 6], P('sector')
Inputs may be any that keep to these rules, and one draw needn't show every extreme that they name: `sph_dest`: within the spheres of one source bin no destination is named by more than 64 spheres, a bound that some block reaches. `body_list`: the 2 bodies of one bin are different. `tile_codes`: the 32 codes of one bin and intersection entry are different. `sph_state`: every radius (row 6) lies between 0.3 and 0.7. `triangles`: for every triangle, |e1 x e2|^2 is at least 0.2.
All inputs are finite; a program needn't handle non-finite values.
Results may differ from a plain program's by a relative error of at most 0.0003.
Values sent between devices are 32-bit elements; how exact they have to be, the bound alone decides.
No kernel may reach another device: no remote copies, remote signals or barrier semaphores. Data moves between devices by JAX's collectives and lax.ppermute only.
A program may use at most 64 MiB of HBM per device.

v0:
```python
import jax
import jax.numpy as jnp
from jax import lax
from jax.sharding import PartitionSpec as P

stiff_pair = 50.0
damp_pair = 2.0
stiff_wall = 50.0
time_step = 0.01
gravity = 9.81
body_mass = 4.0
body_inertia = 40.0


def contact(spheres, facets):
    centre = spheres[0:3]
    radius = spheres[3]
    corner = facets[0:3]
    edge_one = facets[3:6] - corner
    edge_two = facets[6:9] - corner
    square_one = jnp.sum(edge_one * edge_one, 0)
    square_two = jnp.sum(edge_two * edge_two, 0)
    cross_term = jnp.sum(edge_one * edge_two, 0)
    inverse = 1.0 / (square_one * square_two - cross_term * cross_term)
    relative = centre[:, :, None] - corner[:, None, :]
    along_one = jnp.sum(relative * edge_one[:, None, :], 0)
    along_two = jnp.sum(relative * edge_two[:, None, :], 0)
    weight_b = (square_two * along_one - cross_term * along_two) * inverse
    weight_c = (square_one * along_two - cross_term * along_one) * inverse
    weight_a = jnp.maximum(1.0 - weight_b - weight_c, 0.0)
    weight_b = jnp.maximum(weight_b, 0.0)
    weight_c = jnp.maximum(weight_c, 0.0)
    totals = weight_a + weight_b + weight_c
    weight_b = weight_b / totals
    weight_c = weight_c / totals
    nearest = (
        corner[:, None, :]
        + weight_b[None] * edge_one[:, None, :]
        + weight_c[None] * edge_two[:, None, :]
    )
    offset = centre[:, :, None] - nearest
    squared = jnp.sum(offset * offset, 0)
    strength = stiff_wall * jnp.maximum(radius[:, None] * radius[:, None] - squared, 0.0)
    forces = strength[None] * offset
    on_spheres = jnp.sum(forces, 2)
    on_body = -jnp.sum(forces, (1, 2))
    torque = -jnp.sum(jnp.cross(nearest, forces, axis=0), (1, 2))
    return (on_spheres, jnp.concatenate([on_body, torque]))


def tile_forces(spheres, facets, tile_list):
    tiles_tri = facets.shape[1] // 128

    def advance_tile(carried, tile_code):
        forces, wrench = carried
        sphere_tile = tile_code // tiles_tri
        facet_tile = tile_code % tiles_tri
        sphere_part = lax.dynamic_slice_in_dim(spheres, sphere_tile * 128, 128, 1)
        facet_part = lax.dynamic_slice_in_dim(facets, facet_tile * 128, 128, 1)
        on_spheres, on_body = contact(sphere_part, facet_part)
        current = lax.dynamic_slice_in_dim(forces, sphere_tile * 128, 128, 1)
        forces = lax.dynamic_update_slice_in_dim(forces, current + on_spheres, sphere_tile * 128, 1)
        return ((forces, wrench + on_body), None)

    initial = (jnp.zeros((3, spheres.shape[1]), jnp.float32), jnp.zeros((6,), jnp.float32))
    (forces, wrench), unused = lax.scan(advance_tile, initial, tile_list)
    return (forces, wrench)


def sphere_forces(sphere_block):
    position = sphere_block[0:3]
    velocity = sphere_block[3:6]
    radius = sphere_block[6]
    width_all = sphere_block.shape[1]
    occupied = (radius > 0).astype(jnp.float32)
    coords = jnp.concatenate([position, radius[None]], 0)
    baseline = radius * radius - jnp.sum(position * position, 0)
    stacked = jnp.concatenate([position, velocity, jnp.ones((1, width_all), jnp.float32)], 0)
    row_block = 512

    def row_group(row_start):
        coords_rows = lax.dynamic_slice_in_dim(coords, row_start, row_block, 1)
        base_rows = lax.dynamic_slice_in_dim(baseline, row_start, row_block, 0)
        live_rows = lax.dynamic_slice_in_dim(occupied, row_start, row_block, 0)
        inner_products = lax.dot_general(
            coords_rows, coords, (((0,), (0,)), ((), ())), precision=lax.Precision.HIGHEST
        )
        intersection = jnp.maximum(
            base_rows[:, None] + baseline[None, :] + 2.0 * inner_products, 0.0
        )
        intersection = intersection * live_rows[:, None] * occupied[None, :]
        return lax.dot_general(
            stacked, intersection, (((1,), (1,)), ((), ())), precision=lax.Precision.HIGHEST
        )

    starts = jnp.arange(width_all // row_block, dtype=jnp.int32) * row_block
    grouped = lax.map(row_group, starts)
    weighted = jnp.transpose(grouped, (1, 0, 2)).reshape(7, width_all)
    totals = weighted[6]
    return stiff_pair * (totals * position - weighted[0:3]) - damp_pair * (
        totals * velocity - weighted[3:6]
    )


def advance(sphere_block, forces):
    position = sphere_block[0:3]
    velocity = sphere_block[3:6]
    radius = sphere_block[6]
    occupied = radius > 0
    masses = jnp.where(occupied, radius * radius * radius, 1.0)
    falling = jnp.array([0.0, 0.0, gravity], jnp.float32)
    acceleration = forces / masses[None] - falling[:, None]
    velocity_new = velocity + time_step * acceleration
    position_new = position + time_step * velocity_new
    result = jnp.concatenate([position_new, velocity_new, radius[None]], 0)
    return jnp.where(occupied[None], result, 0.0)


def bin_total(partial_row):
    return lax.psum(partial_row, "bin")


def local(sph_state, sph_dest, body_list, tile_codes, triangles):
    sectors = lax.axis_size("sector")
    bins = lax.axis_size("bin")
    ndevices = sectors * bins
    leaving = sph_state.shape[1]
    capacity = 2 * leaving // ndevices
    targets = sph_dest[:, 0]
    onehot = (targets[:, None] == jnp.arange(ndevices, dtype=jnp.int32)[None, :]).astype(jnp.int32)
    ranks = jnp.sum((jnp.cumsum(onehot, 0) - 1) * onehot, 1)
    columns = targets * capacity + ranks
    outgoing = jnp.zeros((7, ndevices * capacity), jnp.float32).at[:, columns].set(sph_state)
    outgoing = outgoing.reshape(7, sectors, bins, capacity)
    arrived = lax.all_to_all(
        lax.all_to_all(outgoing, "sector", split_axis=1, concat_axis=1, tiled=True),
        "bin",
        split_axis=2,
        concat_axis=2,
        tiled=True,
    )
    sphere_block = arrived.reshape(7, ndevices * capacity)
    width_all = sphere_block.shape[1]
    coords = jnp.concatenate([sphere_block[0:3], sphere_block[6:7]], 0)
    pair_total = sphere_forces(sphere_block)
    everyone = lax.all_gather(triangles, "sector", axis=1, tiled=True)
    wall_total = jnp.zeros((3, width_all), jnp.float32)
    partial_value = jnp.zeros((sectors, 6), jnp.float32)
    for slot_index in range(body_list.shape[1]):
        owner_body = body_list[0, slot_index]
        facets = lax.dynamic_index_in_dim(everyone, owner_body, 1, keepdims=False)
        on_spheres, on_body = tile_forces(coords, facets, tile_codes[0, slot_index])
        wall_total = wall_total + on_spheres
        selector = (jnp.arange(sectors, dtype=jnp.int32) == owner_body).astype(jnp.float32)
        partial_value = partial_value + selector[:, None] * on_body[None, :]
    own_row = lax.psum_scatter(partial_value, "sector", scatter_dimension=0, tiled=True)
    own_row = bin_total(own_row)
    new_block = advance(sphere_block, pair_total + wall_total)
    scaling = jnp.array([time_step / body_mass] * 3 + [time_step / body_inertia] * 3, jnp.float32)
    return (new_block, own_row * scaling[None, :])


def solution(mesh):
    return jax.shard_map(
        local,
        mesh=mesh,
        in_specs=(
            P(None, ("sector", "bin")),
            P(("sector", "bin"), None),
            P(("sector", "bin"), None),
            P(("sector", "bin"), None, None),
            P(None, "sector", "bin"),
        ),
        out_specs=(P(None, ("sector", "bin")), P("sector", None)),
        check_vma=False,
    )
```

profile of v0, /device:TPU:0, one launch (start us, length us, event | category | flops | bytes accessed | tf_op | source)
XLA Modules:
  0.0 403.7 jit_solution(1080222455080420332)
XLA Ops:
  0.7 0.7 fusion.46
  1.4 9.0 %reduce-window.6 = s32[32,8,128]{2,1,0:T(8,128)S(1)} reduce-window(s32[32,8,128]{2,1,0:T(8,128)S(1)} %fusion.46, s32[]{:T(128)} %constant.210.clone.1), window={size=1x1x128 pad=0_0x0_0x127_0}, to_apply=%region_0.0 | reduce-window | flops 4161536 | bytes 262148 | tf_op jit(solution)/shard_map/reduce-window
  10.9 0.7 fusion.45
  11.6 0.7 compare_select_fusion
  12.3 1.0 copy.100
  13.3 3.3 scatter_custom_fusion
  17.0 0.8 reshape.697
  17.8 5.2 %all-to-all-start = ((f32[4,1,3584]{2,1,0:T(1,128)}), f32[4,1,3584]{2,1,0:T(1,128)S(1)}, u32[]{:S(2)}, u32[]{:S(2)}) async-start(f32[4,1,3584]{2,1,0:T(1,128)} %reshape.697), calls=%async_computation | async-start | bytes 114688 | tf_op jit(solution)/shard_map/all_to_all | solution.py:136
  23.0 0.6 fusion.51
  26.4 13.4 %all_gather.3 = f32[9,4,4096]{2,0,1:T(8,128)S(1)} all-gather(f32[9,1,4096]{2,0,1:T(8,128)S(1)} %copy.108), channel_id=1, replica_groups=mesh['sector'=4,'bin'=8] {'sector'}, dimensions={1}, use_global_device_ids=true | all-gather | bytes 737280 | tf_op jit(solution)/shard_map/all_gather | solution.py:146
  41.1 1.3 compare_convert_fusion
  42.6 0.7 dynamic-slice
  43.8 0.8 reduce.1
  44.7 0.8 reshape.699
  45.4 4.9 %all-to-all-start.1 = ((f32[8,1,1792]{2,1,0:T(1,128)}), f32[8,1,1792]{2,1,0:T(1,128)S(1)}, u32[]{:S(2)}, u32[]{:S(2)}) async-start(f32[8,1,1792]{2,1,0:T(1,128)} %reshape.699), calls=%async_computation.1 | async-start | bytes 114688 | tf_op jit(solution)/shard_map/all_to_all | solution.py:135
  50.3 5.9 %all-to-all-done.1 = f32[8,1,1792]{2,1,0:T(1,128)S(1)} async-done(((f32[8,1,1792]{2,1,0:T(1,128)}), f32[8,1,1792]{2,1,0:T(1,128)S(1)}, u32[]{:S(2)}, u32[]{:S(2)}) %all-to-all-start.1) | async-done | bytes 57376 | tf_op jit(solution)/shard_map/all_to_all | solution.py:135
  56.2 0.8 reduce.2
  57.7 43.1 %while.40 = (s32[]{:T(128)}, f32[4,7,512]{2,1,0:T(8,128)S(1)}, s32[4]{0:T(128)S(1)}, f32[2048]{0:T(1024)S(1)}, f32[4,2048]{1,0:T(4,128)S(1)}, /*index=5*/f32[204...) while((s32[]{:T(128)}, f32[4,7,512]{2,1,0:T(8,128)S(1)}, s32[4]{0:T(128)S(1)}, ...), condition=%wide.region_6.7_spmd, body=%wide.region_5.6_spmd.sunk | while | flops 144703488 | bytes 8540323 | solution.py:97
  57.7 0.6 dynamic_slice.98
  60.4 3.6 fusion.70
  64.0 4.5 %fusion.71 = f32[4,7,512]{2,1,0:T(8,128)S(1)} fusion(f32[4,7,512]{2,1,0:T(8,128)S(1)} %get-tuple-element.710, s32[]{:T(128)} %get-tuple-element.709, f32[7,2048]{1,0:T(8,128)S(1)} %get-tuple-element.725, f32[512,2048]{1,0:T(8,128)S(1)} %fusion.70, f32[2048]{0:T(1024)S(1)} %get-tuple-element.724, f32[512]{0:T(512)S(1)} %dynamic_slice.99, ...), kind=kOutput, calls=%fused_computation.15.clone.1 | convolution fusion | flops 94371840 | bytes 4296708 | tf_op jit(solution)/shard_map/while/body/eval_jaxpr/dot_general | solution.py:92
  68.5 0.6 dynamic_slice.98
  71.2 3.6 fusion.70
  74.7 4.5 %fusion.71 = f32[4,7,512]{2,1,0:T(8,128)S(1)} fusion(f32[4,7,512]{2,1,0:T(8,128)S(1)} %get-tuple-element.710, s32[]{:T(128)} %get-tuple-element.709, f32[7,2048]{1,0:T(8,128)S(1)} %get-tuple-element.725, f32[512,2048]{1,0:T(8,128)S(1)} %fusion.70, f32[2048]{0:T(1024)S(1)} %get-tuple-element.724, f32[512]{0:T(512)S(1)} %dynamic_slice.99, ...), kind=kOutput, calls=%fused_computation.15.clone.1 | convolution fusion | flops 94371840 | bytes 4296708 | tf_op jit(solution)/shard_map/while/body/eval_jaxpr/dot_general | solution.py:92
  79.2 0.6 dynamic_slice.98
  81.9 3.6 fusion.70
  85.5 4.5 %fusion.71 = f32[4,7,512]{2,1,0:T(8,128)S(1)} fusion(f32[4,7,512]{2,1,0:T(8,128)S(1)} %get-tuple-element.710, s32[]{:T(128)} %get-tuple-element.709, f32[7,2048]{1,0:T(8,128)S(1)} %get-tuple-element.725, f32[512,2048]{1,0:T(8,128)S(1)} %fusion.70, f32[2048]{0:T(1024)S(1)} %get-tuple-element.724, f32[512]{0:T(512)S(1)} %dynamic_slice.99, ...), kind=kOutput, calls=%fused_computation.15.clone.1 | convolution fusion | flops 94371840 | bytes 4296708 | tf_op jit(solution)/shard_map/while/body/eval_jaxpr/dot_general | solution.py:92
  90.0 0.6 dynamic_slice.98
  92.7 3.6 fusion.70
  96.3 4.5 %fusion.71 = f32[4,7,512]{2,1,0:T(8,128)S(1)} fusion(f32[4,7,512]{2,1,0:T(8,128)S(1)} %get-tuple-element.710, s32[]{:T(128)} %get-tuple-element.709, f32[7,2048]{1,0:T(8,128)S(1)} %get-tuple-element.725, f32[512,2048]{1,0:T(8,128)S(1)} %fusion.70, f32[2048]{0:T(1024)S(1)} %get-tuple-element.724, f32[512]{0:T(512)S(1)} %dynamic_slice.99, ...), kind=kOutput, calls=%fused_computation.15.clone.1 | convolution fusion | flops 94371840 | bytes 4296708 | tf_op jit(solution)/shard_map/while/body/eval_jaxpr/dot_general | solution.py:92
  100.8 138.6 %while.42 = (s32[]{:T(128)}, f32[3,2048]{1,0:T(4,128)S(1)}, f32[6]{0:T(128)S(1)}, s32[32]{0:T(128)S(1)}, f32[4,2048]{1,0:T(4,128)S(1)}, /*index=5*/f32[9,4096]{1...) while((s32[]{:T(128)}, f32[3,2048]{1,0:T(4,128)S(1)}, ...), condition=%wide.region_28.30_spmd.clone, body=%wide.region_18.29_spmd.clone.sunk | while | flops 1559858 | bytes 2144390 | solution.py:66
  100.8 0.6 dynamic_slice.106
  105.2 0.6 dynamic_slice.106
  113.8 0.6 dynamic_slice.106
  122.5 0.6 dynamic_slice.106
  126.8 0.6 dynamic_slice.106
  135.5 0.6 dynamic_slice.106
  139.8 0.6 dynamic_slice.106
  148.5 0.6 dynamic_slice.106
  161.5 0.6 dynamic_slice.106
  170.1 0.6 dynamic_slice.106
  174.5 0.6 dynamic_slice.106
  183.1 0.6 dynamic_slice.106
  187.5 0.6 dynamic_slice.106
  196.1 0.6 dynamic_slice.106
  204.8 0.6 dynamic_slice.106
  209.1 0.6 dynamic_slice.106
  217.8 0.6 dynamic_slice.106
  222.1 0.6 dynamic_slice.106
  230.8 0.6 dynamic_slice.106
  239.5 138.7 %while.41 = (s32[]{:T(128)}, f32[3,2048]{1,0:T(4,128)S(1)}, f32[6]{0:T(128)S(1)}, s32[32]{0:T(128)S(1)}, f32[4,2048]{1,0:T(4,128)S(1)}, /*index=5*/f32[9,4096]{1...) while((s32[]{:T(128)}, f32[3,2048]{1,0:T(4,128)S(1)}, ...), condition=%wide.region_17.19_spmd.clone, body=%wide.region_7.18_spmd.clone.sunk | while | flops 1559858 | bytes 2144390 | solution.py:66
  239.5 0.6 dynamic_slice.103
  243.8 0.6 dynamic_slice.103
  252.5 0.6 dynamic_slice.103
  261.1 0.6 dynamic_slice.103
  269.8 0.6 dynamic_slice.103
  274.1 0.6 dynamic_slice.103
  282.8 0.6 dynamic_slice.103
  291.5 0.6 dynamic_slice.103
  295.8 0.6 dynamic_slice.103
  379.0 8.9 %all-reduce = f32[4,6]{1,0:T(4,128)S(1)} all-reduce(f32[4,6]{1,0:T(4,128)S(1)} %multiply_add_fusion.3), channel_id=2, replica_groups=mesh['sector'=4,'bin'=8] {'sector'}, use_global_device_ids=true, to_apply=%region_29.31.clone | all-reduce | flops 24 | bytes 192
  388.0 0.7 constant_dynamic-slice_fusion.4
  388.7 1.0 copy.110
  389.6 13.6 %psum.7 = f32[1,6]{1,0:T(1,128)S(1)} all-reduce(f32[1,6]{1,0:T(1,128)S(1)} %constant_dynamic-slice_fusion.4), channel_id=1, replica_groups=mesh['sector'=4,'bin'=8] {'bin'}, use_global_device_ids=true, to_apply=%region_30.32 | all-reduce | flops 6 | bytes 48 | tf_op jit(solution)/shard_map/psum | solution.py:120
  (1061 shorter events, 92.5 us)
Async XLA Ops:
  0.6 42.0 %copy-start.5 = (u32[32]{0:T(128)S(1)}, u32[32]{0:T(128)}, u32[]{:S(2)}) copy-start(u32[32]{0:T(128)} %constant.228) | copy-start | bytes 388
  0.6 22.3 %copy-start.1 = (s32[1,2]{1,0:T(1,128)S(1)}, s32[1,2]{1,0:T(1,128)}, u32[]{:S(2)}) copy-start(s32[1,2]{1,0:T(1,128)} %param.17) | copy-start | bytes 28
  0.7 25.6 %copy-start = (f32[9,1,4096]{2,1,0:T(1,128)S(1)}, f32[9,1,4096]{2,1,0:T(1,128)}, u32[]{:S(2)}) copy-start(f32[9,1,4096]{2,1,0:T(1,128)} %param.19) | copy-start | bytes 442372
  0.7 39.1 %copy-start.2 = (s32[1,2,32]{2,1,0:T(2,128)S(1)}, s32[1,2,32]{2,1,0:T(2,128)}, u32[]{:S(2)}) copy-start(s32[1,2,32]{2,1,0:T(2,128)} %param.18) | copy-start | bytes 772
  17.8 25.5 %all-to-all-start = ((f32[4,1,3584]{2,1,0:T(1,128)}), f32[4,1,3584]{2,1,0:T(1,128)S(1)}, u32[]{:S(2)}, u32[]{:S(2)}) async-start(f32[4,1,3584]{2,1,0:T(1,128)} %reshape.697), calls=%async_computation | async-start | bytes 114688 | tf_op jit(solution)/shard_map/all_to_all | solution.py:136
  45.4 10.8 %all-to-all-start.1 = ((f32[8,1,1792]{2,1,0:T(1,128)}), f32[8,1,1792]{2,1,0:T(1,128)S(1)}, u32[]{:S(2)}, u32[]{:S(2)}) async-start(f32[8,1,1792]{2,1,0:T(1,128)} %reshape.699), calls=%async_computation.1 | async-start | bytes 114688 | tf_op jit(solution)/shard_map/all_to_all | solution.py:135
  239.4 138.7 %copy-start.3 = (f32[3]{0:T(128)S(1)}, f32[3]{0:T(128)}, u32[]{:S(2)}) copy-start(f32[3]{0:T(128)} %constant.224) | copy-start | bytes 40
  378.1 25.1 %copy-start.4 = (f32[1,6]{1,0:T(1,128)S(1)}, f32[1,6]{1,0:T(1,128)}, u32[]{:S(2)}) copy-start(f32[1,6]{1,0:T(1,128)} %constant.225) | copy-start | bytes 76
where the time goes:
time: 408 us; the launch traced here: 404 us
  loops' own time  181 us (44%)
  other arithmetic  81.9 us (20%)
  local copies, waits for them, and re-layouts  52.1 us (13%)
  blocking collectives  35.9 us (9%)
  matrix products  32.2 us (8%)
  starting transfers between devices  10.1 us (2%)
  waiting for transfers between devices  5.87 us (1%)
  between operations  4.95 us (1%)
    another operation x2, loops' own time, tile_forces(): (forces, wrench), unused = lax.scan(advance_tile, initial, tile_list)  173 us
    dynamic_slice x64, local copies, waits for them, and re-layouts, tile_forces(): (forces, wrench), unused = lax.scan(advance_tile, initial, tile_list)  37.3 us
    reduce_sum x64, other arithmetic, contact(): on_body = -jnp.sum(forces, (1, 2))  19.1 us
    dot_general x4, matrix products, row_group(): lax.dot_general(stacked, intersection, (((1,), (1,)), ((), ())), precisio...  17.9 us
    dot_general x4, matrix products, row_group(): lax.dot_general(coords_rows, coords, (((0,), (0,)), ((), ())), precision=...  14.3 us
    psum x1, blocking collectives, bin_total(): return lax.psum(partial_row, 'bin')  13.6 us
    all_gather x1, blocking collectives, local(): everyone = lax.all_gather(triangles, 'sector', axis=1, tiled=True)  13.4 us
    another operation x2, other arithmetic  9.04 us
  transfers between devices with their start and end apart: 2, of which 1 were waited for; matrix products, arithmetic and copies ran while one was open for 1% of the time, Pallas kernels for 0%

commit v1 on v0

--- a/solution.py
+++ b/solution.py
@@ -1,6 +1,10 @@
+import functools
+
 import jax
 import jax.numpy as jnp
 from jax import lax
+from jax.experimental import pallas as pl
+from jax.experimental.pallas import tpu as pltpu
 from jax.sharding import PartitionSpec as P
 
 stiff_pair = 50.0
@@ -10,6 +14,322 @@
 gravity = 9.81
 body_mass = 4.0
 body_inertia = 40.0
+
+LANES = 128
+PAYLOAD = ((0, 3), (1, 4), (2, 5), (6, None))
+PAIR_BLOCK = 256
+WALL_ROWS = 128
+
+
+def iota(shape, dim):
+    return lax.broadcasted_iota(jnp.int32, shape, dim)
+
+
+def split3(x):
+    hi = x.astype(jnp.bfloat16).astype(jnp.float32)
+    rest = x - hi
+    mid = rest.astype(jnp.bfloat16).astype(jnp.float32)
+    return hi, mid, rest - mid
+
+
+def dot(a, b, contract=((1,), (0,))):
+    return lax.dot_general(a, b, (contract, ((), ())), preferred_element_type=jnp.float32)
+
+
+def pack_kernel(dest_ref, state_ref, out_ref):
+    blocks = dest_ref.shape[0]
+    ndevices = out_ref.shape[0] * LANES // (8 * 64)
+    capacity = 64
+    dest = dest_ref[...]
+    wide = blocks * ndevices
+    expand = (iota((blocks, wide), 1) // ndevices == iota((blocks, wide), 0)).astype(jnp.bfloat16)
+    dest_cols = jnp.transpose(dest.astype(jnp.float32)).astype(jnp.bfloat16)
+    named = dot(dest_cols, expand)
+    onehot = (named == (iota((LANES, wide), 1) % ndevices).astype(jnp.float32)).astype(jnp.float32)
+    lower = (iota((LANES, LANES), 0) >= iota((LANES, LANES), 1)).astype(jnp.bfloat16)
+    counted = dot(lower, onehot.astype(jnp.bfloat16))
+    total = jnp.broadcast_to(counted[LANES - 1 :], (8, wide))
+    before = jnp.zeros((8, wide), jnp.float32)
+    for step in range(1, blocks):
+        moved = pltpu.roll(total, step * ndevices, 1)
+        before = before + jnp.where(iota((8, wide), 1) >= step * ndevices, moved, 0.0)
+    place = (onehot * (counted - 1.0 + before[0:1])).astype(jnp.bfloat16)
+    ranks = dot(expand, place, ((1,), (1,)))
+    rank_row = jnp.concatenate([ranks[b : b + 1] for b in range(blocks)], 1)
+    dest_row = jnp.concatenate([dest[b : b + 1] for b in range(blocks)], 1)
+    leaving = blocks * LANES
+    chosen = rank_row == iota((capacity, leaving), 0).astype(jnp.float32)
+    to_dest = (dest_row == iota((ndevices, leaving), 0)).astype(jnp.float32).astype(jnp.bfloat16)
+    out = None
+    for part in split3(state_ref[...]):
+        rows = []
+        for pair in PAYLOAD:
+            for source in pair:
+                if source is None:
+                    rows.append(jnp.zeros((capacity, leaving), jnp.bfloat16))
+                else:
+                    rows.append(jnp.where(chosen, part[source : source + 1], 0.0).astype(jnp.bfloat16))
+        piece = dot(to_dest, jnp.concatenate(rows, 0), ((1,), (1,)))
+        out = piece if out is None else out + piece
+    groups = len(PAYLOAD)
+    for k in range(groups):
+        out_ref[pl.ds(k, ndevices, stride=groups), :] = out[:, k * LANES : (k + 1) * LANES]
+
+
+def total_of(x):
+    return jnp.sum(jnp.sum(x, 0, keepdims=True), 1, keepdims=True)
+
+
+def state_tile(arrived_ref, tile):
+    words = arrived_ref[8 * tile : 8 * tile + 8, :]
+    swapped = pltpu.roll(pltpu.roll(words, 64, 1), 4, 0)
+    same = (iota((8, LANES), 0) < 4) == (iota((8, LANES), 1) < 64)
+    return jnp.where(same, words, swapped)
+
+
+def wall_kernel(sectors, bins, *refs):
+    tri_refs = refs[2 : 2 + sectors]
+    bodies_ref, codes_ref = refs[0:2]
+    entries = bodies_ref.shape[1]
+    arrived_ref = refs[2 + sectors]
+    wrench_ref, force_ref = refs[3 + sectors : 5 + sectors]
+    raw, facet, px, py, pz, rr, place, gathered, tri_sem = refs[5 + sectors : 14 + sectors]
+    accs = refs[14 + sectors :]
+    codes = codes_ref.shape[2]
+    tiles_tri = raw.shape[2]
+    tiles = arrived_ref.shape[0] // 8
+    me = lax.axis_index("sector")
+
+    def fetch(entry, source):
+        return pltpu.make_async_copy(tri_refs[source], raw.at[entry], tri_sem.at[entry])
+
+    for entry in range(entries):
+        relative = bodies_ref[0, entry] ^ me
+        for source in range(sectors):
+
+            @pl.when(relative == source)
+            def _():
+                fetch(entry, source).start()
+
+    turned = jnp.transpose(arrived_ref[...])[0:64]
+    squared = turned * turned
+    for q in range(2 * tiles):
+        at = slice(64 * q, 64 * q + 64)
+        for ref, source, i in ((px, turned, 0), (py, turned, 1), (pz, turned, 2), (rr, squared, 3)):
+            lane = 4 * q + i
+            ref[at, :] = jnp.broadcast_to(source[:, lane : lane + 1], (64, LANES))
+    for tile in range(tiles):
+        state = state_tile(arrived_ref, tile)
+        for i in range(3):
+            place[i, tile : tile + 1, :] = state[i : i + 1]
+
+    for acc in accs:
+        acc[...] = jnp.zeros_like(acc)
+
+    for entry in range(entries):
+        fetch(entry, 0).wait()
+        corner = [raw[entry, i] for i in range(3)]
+        one = [raw[entry, 3 + i] - corner[i] for i in range(3)]
+        two = [raw[entry, 6 + i] - corner[i] for i in range(3)]
+        d11 = one[0] * one[0] + one[1] * one[1] + one[2] * one[2]
+        d12 = one[0] * two[0] + one[1] * two[1] + one[2] * two[2]
+        d22 = two[0] * two[0] + two[1] * two[1] + two[2] * two[2]
+        inverse = 1.0 / (d11 * d22 - d12 * d12)
+        for i in range(3):
+            facet[entry, i] = corner[i]
+            facet[entry, 3 + i] = one[i]
+            facet[entry, 6 + i] = two[i]
+            facet[entry, 9 + i] = (d22 * one[i] - d12 * two[i]) * inverse
+            facet[entry, 12 + i] = (d11 * two[i] - d12 * one[i]) * inverse
+
+    def one_tile(entry, number):
+        code = codes_ref[0, entry, number]
+        first = pl.multiple_of(code // tiles_tri * LANES, LANES)
+        facet_tile = code % tiles_tri
+        f = [facet[entry, i, pl.ds(facet_tile, 1), :] for i in range(15)]
+        for part in range(LANES // WALL_ROWS):
+            at = pl.ds(pl.multiple_of(first + part * WALL_ROWS, WALL_ROWS), WALL_ROWS)
+            dx, dy, dz = px[at, :] - f[0], py[at, :] - f[1], pz[at, :] - f[2]
+            beta = dx * f[9] + dy * f[10] + dz * f[11]
+            gamma = dx * f[12] + dy * f[13] + dz * f[14]
+            alpha = jnp.maximum(1.0 - beta - gamma, 0.0)
+            beta = jnp.maximum(beta, 0.0)
+            gamma = jnp.maximum(gamma, 0.0)
+            scale = 1.0 / (alpha + beta + gamma)
+            beta = beta * scale
+            gamma = gamma * scale
+            ox = dx - beta * f[3] - gamma * f[6]
+            oy = dy - beta * f[4] - gamma * f[7]
+            oz = dz - beta * f[5] - gamma * f[8]
+            deep = jnp.maximum(rr[at, :] - (ox * ox + oy * oy + oz * oz), 0.0)
+            accs[3 * entry][at, :] += deep * ox
+            accs[3 * entry + 1][at, :] += deep * oy
+            accs[3 * entry + 2][at, :] += deep * oz
+
+    def step(number, carry):
+        for entry in range(entries):
+            one_tile(entry, number)
+        return carry
+
+    lax.fori_loop(0, codes, step, 0)
+
+    def gather(tile, carry):
+        at = pl.ds(pl.multiple_of(tile * LANES, LANES), LANES)
+        for which in range(3 * entries):
+            row = jnp.sum(jnp.transpose(accs[which][at, :]), 0, keepdims=True)
+            gathered[which, pl.ds(tile, 1), :] = row
+        return carry
+
+    lax.fori_loop(0, tiles, gather, 0)
+    x, y, z = place[0], place[1], place[2]
+    owner = iota((sectors * bins, LANES), 0) // bins
+    lane = iota((1, LANES), 1)
+    out = jnp.zeros((sectors * bins, LANES), jnp.float32)
+    whole = [0.0, 0.0, 0.0]
+    for entry in range(entries):
+        fx, fy, fz = (gathered[3 * entry + i] for i in range(3))
+        parts = (fx, fy, fz, y * fz - z * fy, z * fx - x * fz, x * fy - y * fx)
+        mine = jnp.zeros((1, LANES), jnp.float32)
+        for i, part in enumerate(parts):
+            mine = jnp.where(lane == i, total_of(part), mine)
+        out = out + jnp.where(owner == bodies_ref[0, entry], mine * (-stiff_wall), 0.0)
+        whole = [whole[0] + fx, whole[1] + fy, whole[2] + fz]
+    wrench_ref[...] = out
+    for i in range(3):
+        force_ref[i] = stiff_wall * whole[i]
+
+
+def pair_kernel(arrived_ref, force_ref, out_ref, left, right, moved):
+    tiles = arrived_ref.shape[0] // 8
+    blocks = tiles * LANES // PAIR_BLOCK
+    row8 = iota((8, LANES), 0)
+    for tile in range(tiles):
+        at = slice(tile * LANES, (tile + 1) * LANES)
+        state = state_tile(arrived_ref, tile)
+        square = state * state
+        level = square[3:4] - (square[0:1] + square[1:2] + square[2:3])
+        other = jnp.where(state[3:4] > 0.0, level, -3.0e38)
+        i_side = jnp.where(row8 < 4, 2.0 * state, jnp.where(row8 == 4, level, jnp.where(row8 == 5, 1.0, 0.0)))
+        j_side = jnp.where(row8 < 4, state, jnp.where(row8 == 4, 1.0, jnp.where(row8 == 5, other, 0.0)))
+        ih, im, il = split3(i_side)
+        jh, jm, jl = split3(j_side)
+        right[:, at] = jnp.concatenate([ih, ih, im, ih, il, im], 0).astype(jnp.bfloat16)
+        left[at, 0:48] = jnp.transpose(jnp.concatenate([jh, jm, jh, jl, jh, jm], 0)).astype(jnp.bfloat16)
+        value = jnp.where(row8 == 3, 1.0, state)
+        moved[:, at] = jnp.concatenate(list(split3(value)) + [jnp.zeros((8, LANES), jnp.float32)], 0).astype(
+            jnp.bfloat16
+        )
+
+    def block_of(ib, carry):
+        columns = pl.ds(pl.multiple_of(ib * PAIR_BLOCK, PAIR_BLOCK), PAIR_BLOCK)
+        mine = right[:, columns]
+        total = jnp.zeros((32, PAIR_BLOCK), jnp.float32)
+        for jb in range(blocks):
+            rows = slice(jb * PAIR_BLOCK, (jb + 1) * PAIR_BLOCK)
+            weight = jnp.maximum(dot(left[rows, 0:48], mine), 0.0)
+            high = weight.astype(jnp.bfloat16)
+            low = (weight - high.astype(jnp.float32)).astype(jnp.bfloat16)
+            values = moved[:, rows]
+            total = total + (dot(values, high) + dot(values, low))
+        total = total[0:8] + total[8:16] + total[16:24]
+        for part in range(PAIR_BLOCK // LANES):
+            tile = ib * (PAIR_BLOCK // LANES) + part
+            words = arrived_ref[pl.ds(pl.multiple_of(8 * tile, 8), 8), :]
+            swapped = pltpu.roll(pltpu.roll(words, 64, 1), 4, 0)
+            state = jnp.where((row8 < 4) == (iota((8, LANES), 1) < 64), words, swapped)
+            moment = total[:, part * LANES : (part + 1) * LANES]
+            differ = moment[3:4] * state - moment
+            force = stiff_pair * differ - damp_pair * pltpu.roll(differ, 4, 0)
+            for i in range(3):
+                force = force + jnp.where(row8 == i, force_ref[i, pl.ds(tile, 1), :], 0.0)
+            radius = jnp.broadcast_to(state[3:4], (8, LANES))
+            live = radius > 0.0
+            mass = jnp.where(live, radius * radius * radius, 1.0)
+            falling = jnp.where(row8 == 6, gravity, 0.0)
+            speed = state + time_step * (pltpu.roll(force, 4, 0) / mass - falling)
+            place = state + time_step * pltpu.roll(speed, 4, 0)
+            result = jnp.where(
+                row8 < 3, place, jnp.where(row8 < 6, pltpu.roll(speed, 7, 0), pltpu.roll(state, 3, 0))
+            )
+            result = jnp.where(live, result, 0.0)
+            out_ref[:, pl.ds(pl.multiple_of(tile * LANES, LANES), LANES)] = result[0:7]
+        return carry
+
+    lax.fori_loop(0, blocks, block_of, 0)
+
+
+def whole_vmem():
+    return pl.BlockSpec(memory_space=pltpu.VMEM)
+
+
+def whole_smem():
+    return pl.BlockSpec(memory_space=pltpu.SMEM)
+
+
+def fast(sph_state, sph_dest, body_list, tile_codes, triangles):
+    sectors = lax.axis_size("sector")
+    bins = lax.axis_size("bin")
+    ndevices = sectors * bins
+    leaving = sph_state.shape[1]
+    slots = 2 * leaving
+    words = 8 * slots // LANES
+    block = triangles.reshape(triangles.shape[0], -1, LANES)
+    blocks = [block] + [
+        lax.ppermute(block, "sector", [(i, i ^ step) for i in range(sectors)]) for step in range(1, sectors)
+    ]
+    outgoing = pl.pallas_call(
+        pack_kernel,
+        out_shape=jax.ShapeDtypeStruct((words, LANES), jnp.float32),
+        in_specs=[whole_vmem(), whole_vmem()],
+        out_specs=whole_vmem(),
+        name="pack",
+    )(sph_dest.reshape(-1, LANES), sph_state)
+    outgoing = outgoing.reshape(ndevices, 1, words * LANES // ndevices)
+    arrived = lax.all_to_all(outgoing, ("sector", "bin"), split_axis=0, concat_axis=0, tiled=True)
+    arrived = arrived.reshape(words, LANES)
+    entries = body_list.shape[1]
+    column = pltpu.VMEM((slots, LANES), jnp.float32)
+    tiles = slots // LANES
+    wrench, force = pl.pallas_call(
+        functools.partial(wall_kernel, sectors, bins),
+        out_shape=[
+            jax.ShapeDtypeStruct((ndevices, LANES), jnp.float32),
+            jax.ShapeDtypeStruct((3, tiles, LANES), jnp.float32),
+        ],
+        in_specs=[whole_smem(), whole_smem()] + [pl.BlockSpec(memory_space=pl.ANY)] * sectors + [whole_vmem()],
+        out_specs=[whole_vmem()] * 2,
+        scratch_shapes=[
+            pltpu.VMEM((entries,) + block.shape, jnp.float32),
+            pltpu.VMEM((entries, 15) + block.shape[1:], jnp.float32),
+            column,
+            column,
+            column,
+            column,
+            pltpu.VMEM((3, tiles, LANES), jnp.float32),
+            pltpu.VMEM((3 * entries, tiles, LANES), jnp.float32),
+            pltpu.SemaphoreType.DMA((entries,)),
+        ]
+        + [column] * (3 * entries),
+        name="wall",
+    )(body_list, tile_codes, *blocks, arrived)
+    shared = lax.all_to_all(
+        wrench.reshape(ndevices, 1, LANES), ("sector", "bin"), split_axis=0, concat_axis=0, tiled=True
+    )
+    new_block = pl.pallas_call(
+        pair_kernel,
+        out_shape=jax.ShapeDtypeStruct((7, slots), jnp.float32),
+        in_specs=[whole_vmem(), whole_vmem()],
+        out_specs=whole_vmem(),
+        scratch_shapes=[
+            pltpu.VMEM((slots, LANES), jnp.bfloat16),
+            pltpu.VMEM((48, slots), jnp.bfloat16),
+            pltpu.VMEM((32, slots), jnp.bfloat16),
+        ],
+        name="pair",
+    )(arrived, force)
+    scaling = jnp.array([time_step / body_mass] * 3 + [time_step / body_inertia] * 3, jnp.float32)
+    kick = jnp.sum(shared[:, 0, :6], 0, keepdims=True) * scaling[None, :]
+    return new_block, kick
 
 
 def contact(spheres, facets):
@@ -120,7 +440,7 @@
     return lax.psum(partial_row, "bin")
 
 
-def local(sph_state, sph_dest, body_list, tile_codes, triangles):
+def general(sph_state, sph_dest, body_list, tile_codes, triangles):
     sectors = lax.axis_size("sector")
     bins = lax.axis_size("bin")
     ndevices = sectors * bins
@@ -160,6 +480,15 @@
     return (new_block, own_row * scaling[None, :])
 
 
+def local(sph_state, sph_dest, body_list, tile_codes, triangles):
+    sectors = lax.axis_size("sector")
+    ndevices = sectors * lax.axis_size("bin")
+    leaving = sph_state.shape[1]
+    fits = 2 * leaving == 64 * ndevices and 16 * leaving == LANES * LANES and sectors & (sectors - 1) == 0
+    chosen = fast if fits else general
+    return chosen(sph_state, sph_dest, body_list, tile_codes, triangles)
+
+
 def solution(mesh):
     return jax.shard_map(
         local,

time: 408 us -> 49.6 us (0.12)
  loops' own time: 181 us -> 0 us
  other arithmetic: 81.9 us -> 0.56 us
  local copies, waits for them, and re-layouts: 52.1 us -> 1.32 us
  matrix products: 32.2 us -> 0 us
  Pallas kernels: 0 us -> 25.7 us
  blocking collectives: 35.9 us -> 13.7 us
  waiting for transfers between devices: 5.87 us -> 0.01 us
  between operations: 4.95 us -> 0.68 us
    another operation x3 -> x0, loops' own time: 181 us -> none  [the longest x2 173 us: tile_forces(): (forces, wrench), unused = lax.scan(advance_tile, initial, tile_list)]
    reduce_sum x322 -> x1, other arithmetic: 49.6 us -> 0.05 us  [fast(): kick = jnp.sum(shared[:, 0, :6], 0, keepdims=True) * scaling[None, :]]
    dynamic_slice x140 -> x0, local copies, waits for them, and re-layouts: 40.9 us -> none  [the longest x64 37.3 us: tile_forces(): (forces, wrench), unused = lax.scan(advance_tile, initial, tile_list)]
    dot_general x8 -> x0, matrix products: 32.2 us -> none  [the longest x4 17.9 us: row_group(): lax.dot_general(stacked, intersection, (((1,), (1,)), ((), ())), precisio...]
    pallas_call x0 -> x3, Pallas kernels: none -> 25.7 us  [the longest x1 13.8 us: fast(): pl.pallas_call(functools.partial(wall_kernel, sectors, bins), out_shape=[...]
    all_to_all x0 -> x1, blocking collectives: none -> 13.7 us  [fast(): lax.all_to_all(outgoing, ('sector', 'bin'), split_axis=0, concat_axis=0,...]
    psum x1 -> x0, blocking collectives: 13.6 us -> none  [bin_total(): return lax.psum(partial_row, 'bin')]
    all_gather x1 -> x0, blocking collectives: 13.4 us -> none  [local(): everyone = lax.all_gather(triangles, 'sector', axis=1, tiled=True)]
  transfers between devices with their start and end apart: 2 -> 4, of which waited for: 1 -> 0; matrix products, arithmetic and copies ran while one was open for 1% -> 0% of each run, Pallas kernels for 0% -> 24%
where the time goes in v1:
time: 49.6 us; the launch traced here: 49.2 us
  Pallas kernels  25.7 us (52%)
  blocking collectives  13.7 us (28%)
  starting transfers between devices  7.19 us (14%)
  local copies, waits for them, and re-layouts  1.32 us (3%)
  between operations  0.68 us (1%)
  other arithmetic  0.56 us (1%)
    pallas_call x1, Pallas kernels, fast(): pl.pallas_call(functools.partial(wall_kernel, sectors, bins), out_shape=[...  13.8 us
    all_to_all x1, blocking collectives, fast(): lax.all_to_all(outgoing, ('sector', 'bin'), split_axis=0, concat_axis=0,...  13.7 us
    pallas_call x1, Pallas kernels, fast(): pl.pallas_call(pair_kernel, out_shape=jax.ShapeDtypeStruct((7, slots), jn...  9.01 us
    ppermute x3, starting transfers between devices, fast(): lax.ppermute(block, 'sector', [(i, i ^ step) for i in range(sectors)])  4.63 us
    pallas_call x1, Pallas kernels, fast(): pl.pallas_call(pack_kernel, out_shape=jax.ShapeDtypeStruct((words, LANES)...  2.91 us
    all_to_all x1, starting transfers between devices, fast(): lax.all_to_all(wrench.reshape(ndevices, 1, LANES), ('sector', 'bin'), spl...  2.56 us
    unnamed x8, local copies, waits for them, and re-layouts  1.32 us
  transfers between devices with their start and end apart: 4, of which 0 were waited for; matrix products, arithmetic and copies ran while one was open for 0% of the time, Pallas kernels for 24%

profile of v1, /device:TPU:0, one launch (start us, length us, event | category | flops | bytes accessed | tf_op | source)
XLA Modules:
  0.0 49.2 jit_solution(11993351598693548729)
XLA Ops:
  0.6 4.0 %collective-permute-start.2 = (f32[9,32,128]{2,1,0:T(8,128)}, f32[9,32,128]{2,1,0:T(8,128)S(1)}, u32[]{:S(2)}, u32[]{:S(2)}) collective-permute-start(f32[9,32,128]{2,1,0:T(8,128)} %bitcast.12), channel_id=1, source_target_pairs={{0,24},{8,16},{16,8},{24,0},{1,25},{9,17},{17,9},{25,1},{2,26},{10... | collective-permute-start | bytes 442376 | tf_op jit(solution)/shard_map/ppermute | solution.py:278
  4.6 0.5 %collective-permute-start.1 = (f32[9,32,128]{2,1,0:T(8,128)}, f32[9,32,128]{2,1,0:T(8,128)S(1)}, u32[]{:S(2)}, u32[]{:S(2)}) collective-permute-start(f32[9,32,128]{2,1,0:T(8,128)} %bitcast.13), channel_id=1, source_target_pairs={{0,16},{8,24},{16,0},{24,8},{1,17},{9,25},{17,1},{25,9},{2,18},{10... | collective-permute-start | bytes 442376 | tf_op jit(solution)/shard_map/ppermute | solution.py:278
  5.1 0.1 collective-permute-start
  5.3 2.9 %pack.1 = f32[128,128]{1,0:T(8,128)} custom-call(s32[8,128]{1,0:T(8,128)} %bitcast.17, f32[7,1024]{1,0:T(8,128)} %state_ref.1), custom_call_target="tpu_custom_call" | custom-call | tf_op jit(solution)/shard_map/pack/pallas_call | solution.py:280
  8.2 13.7 %all_to_all.10 = f32[32,1,512]{2,1,0:T(1,128)} all-to-all(f32[32,1,512]{2,1,0:T(1,128)} %bitcast.11), channel_id=1, replica_groups=mesh['sector'=4,'bin'=8] {'sector','bin'}, dimensions={0} | all-to-all | bytes 131072 | tf_op jit(solution)/shard_map/all_to_all | solution.py:288
  21.9 0.0 collective-permute-done.2.refs_5_
  21.9 0.0 copy-start
  21.9 0.0 collective-permute-done.1.refs_4_
  21.9 0.0 copy-start.1
  21.9 0.0 collective-permute-done.refs_3_
  21.9 0.0 copy-start.2
  22.0 0.6 %copy-done = f32[9,32,128]{2,1,0:T(8,128)} copy-done((f32[9,32,128]{2,1,0:T(8,128)}, f32[9,32,128]{2,1,0:T(8,128)S(1)}, u32[]{:S(2)}) %copy-start) | copy-done | bytes 147480
  22.6 0.1 copy-done.1
  22.6 0.0 copy-done.2
  22.7 13.8 %wall.1 = (f32[32,128]{1,0:T(8,128)}, f32[3,16,128]{2,1,0:T(8,128)}) custom-call(s32[1,2]{1,0:T(1,128)} %refs_0_.1, s32[1,2,32]{2,1,0:T(2,128)} %refs_1_.1, f32[9,32,128]{2,1,0:T(8,128)} %bitcast.15, f32[9,32,128]{2,1,0:T(8,128)} %copy-done.2, f32[9,32,128]{2,1,0:T(8,128)} %copy-done.1, f32[9,32,128]{2,1,0:T(8,128)} %copy-done, f32[128,128]{1,0:T(8,128)} %bitcast.9), custom_call_target="tpu_custom_call" | custom-call | tf_op jit(solution)/shard_map/wall/pallas_call | solution.py:293
  36.5 2.6 %all-to-all-start.1 = ((f32[32,1,128]{2,1,0:T(1,128)}), f32[32,1,128]{2,1,0:T(1,128)S(1)}, u32[]{:S(2)}, u32[]{:S(2)}) async-start(f32[32,1,128]{2,1,0:T(1,128)} %bitcast.16), calls=%async_computation.1 | async-start | bytes 32768 | tf_op jit(solution)/shard_map/all_to_all | solution.py:315
  39.0 9.0 %pair.1 = f32[7,2048]{1,0:T(8,128)} custom-call(f32[128,128]{1,0:T(8,128)} %bitcast.10, f32[3,16,128]{2,1,0:T(8,128)} %get-tuple-element.4.force_ref), custom_call_target="tpu_custom_call" | custom-call | tf_op jit(solution)/shard_map/pair/pallas_call | solution.py:318
  48.0 0.0 copy-start.3
  48.0 0.0 all-to-all-done.1
  48.0 0.1 slice_reduce_fusion
  48.1 0.6 %copy-done.3 = f32[6]{0:T(128)S(1)} copy-done((f32[6]{0:T(128)S(1)}, f32[6]{0:T(128)}, u32[]{:S(2)}) %copy-start.3) | copy-done | bytes 48
  48.7 0.5 %multiply_bitcast_fusion = f32[1,6]{1,0:T(1,128)} fusion(f32[6]{0:T(128)S(1)} %slice_reduce_fusion, f32[6]{0:T(128)S(1)} %copy-done.3), kind=kLoop, calls=%fused_computation.1 | loop fusion | flops 6 | bytes 72 | tf_op jit(solution)/shard_map/mul | solution.py:331
Async XLA Ops:
  0.6 21.3 %collective-permute-start.2 = (f32[9,32,128]{2,1,0:T(8,128)}, f32[9,32,128]{2,1,0:T(8,128)S(1)}, u32[]{:S(2)}, u32[]{:S(2)}) collective-permute-start(f32[9,32,128]{2,1,0:T(8,128)} %bitcast.12), channel_id=1, source_target_pairs={{0,24},{8,16},{16,8},{24,0},{1,25},{9,17},{17,9},{25,1},{2,26},{10... | collective-permute-start | bytes 442376 | tf_op jit(solution)/shard_map/ppermute | solution.py:278
  4.6 17.3 %collective-permute-start.1 = (f32[9,32,128]{2,1,0:T(8,128)}, f32[9,32,128]{2,1,0:T(8,128)S(1)}, u32[]{:S(2)}, u32[]{:S(2)}) collective-permute-start(f32[9,32,128]{2,1,0:T(8,128)} %bitcast.13), channel_id=1, source_target_pairs={{0,16},{8,24},{16,0},{24,8},{1,17},{9,25},{17,1},{25,9},{2,18},{10... | collective-permute-start | bytes 442376 | tf_op jit(solution)/shard_map/ppermute | solution.py:278
  5.1 16.8 %collective-permute-start = (f32[9,32,128]{2,1,0:T(8,128)}, f32[9,32,128]{2,1,0:T(8,128)S(1)}, u32[]{:S(2)}, u32[]{:S(2)}) collective-permute-start(f32[9,32,128]{2,1,0:T(8,128)} %bitcast.14), channel_id=1, source_target_pairs={{0,8},{8,0},{16,24},{24,16},{1,9},{9,1},{17,25},{25,17},{2,10},{10... | collective-permute-start | bytes 442376 | tf_op jit(solution)/shard_map/ppermute | solution.py:278
  21.9 0.7 %copy-start = (f32[9,32,128]{2,1,0:T(8,128)}, f32[9,32,128]{2,1,0:T(8,128)S(1)}, u32[]{:S(2)}) copy-start(f32[9,32,128]{2,1,0:T(8,128)S(1)} %collective-permute-done.2.refs_5_) | copy-start | bytes 442372
  21.9 0.7 %copy-start.1 = (f32[9,32,128]{2,1,0:T(8,128)}, f32[9,32,128]{2,1,0:T(8,128)S(1)}, u32[]{:S(2)}) copy-start(f32[9,32,128]{2,1,0:T(8,128)S(1)} %collective-permute-done.1.refs_4_) | copy-start | bytes 442372
  21.9 0.7 %copy-start.2 = (f32[9,32,128]{2,1,0:T(8,128)}, f32[9,32,128]{2,1,0:T(8,128)S(1)}, u32[]{:S(2)}) copy-start(f32[9,32,128]{2,1,0:T(8,128)S(1)} %collective-permute-done.refs_3_) | copy-start | bytes 442372
  36.5 11.6 %all-to-all-start.1 = ((f32[32,1,128]{2,1,0:T(1,128)}), f32[32,1,128]{2,1,0:T(1,128)S(1)}, u32[]{:S(2)}, u32[]{:S(2)}) async-start(f32[32,1,128]{2,1,0:T(1,128)} %bitcast.16), calls=%async_computation.1 | async-start | bytes 32768 | tf_op jit(solution)/shard_map/all_to_all | solution.py:315
  48.0 0.7 %copy-start.3 = (f32[6]{0:T(128)S(1)}, f32[6]{0:T(128)}, u32[]{:S(2)}) copy-start(f32[6]{0:T(128)} %constant.4.clone) | copy-start | bytes 76

commit v2 on v1

--- a/solution.py
+++ b/solution.py
@@ -87,17 +87,11 @@
     return jnp.where(same, words, swapped)
 
 
-def wall_kernel(sectors, bins, *refs):
-    tri_refs = refs[2 : 2 + sectors]
-    bodies_ref, codes_ref = refs[0:2]
+def facet_kernel(sectors, *refs):
+    bodies_ref = refs[0]
+    tri_refs = refs[1 : 1 + sectors]
+    facet, raw, tri_sem = refs[1 + sectors :]
     entries = bodies_ref.shape[1]
-    arrived_ref = refs[2 + sectors]
-    wrench_ref, force_ref = refs[3 + sectors : 5 + sectors]
-    raw, facet, px, py, pz, rr, place, gathered, tri_sem = refs[5 + sectors : 14 + sectors]
-    accs = refs[14 + sectors :]
-    codes = codes_ref.shape[2]
-    tiles_tri = raw.shape[2]
-    tiles = arrived_ref.shape[0] // 8
     me = lax.axis_index("sector")
 
     def fetch(entry, source):
@@ -110,21 +104,6 @@
             @pl.when(relative == source)
             def _():
                 fetch(entry, source).start()
-
-    turned = jnp.transpose(arrived_ref[...])[0:64]
-    squared = turned * turned
-    for q in range(2 * tiles):
-        at = slice(64 * q, 64 * q + 64)
-        for ref, source, i in ((px, turned, 0), (py, turned, 1), (pz, turned, 2), (rr, squared, 3)):
-            lane = 4 * q + i
-            ref[at, :] = jnp.broadcast_to(source[:, lane : lane + 1], (64, LANES))
-    for tile in range(tiles):
-        state = state_tile(arrived_ref, tile)
-        for i in range(3):
-            place[i, tile : tile + 1, :] = state[i : i + 1]
-
-    for acc in accs:
-        acc[...] = jnp.zeros_like(acc)
 
     for entry in range(entries):
         fetch(entry, 0).wait()
@@ -141,6 +120,30 @@
             facet[entry, 6 + i] = two[i]
             facet[entry, 9 + i] = (d22 * one[i] - d12 * two[i]) * inverse
             facet[entry, 12 + i] = (d11 * two[i] - d12 * one[i]) * inverse
+
+
+def wall_kernel(sectors, bins, *refs):
+    bodies_ref, codes_ref, facet, arrived_ref, wrench_ref, force_ref, px, py, pz, rr, place, gathered = refs[:12]
+    accs = refs[12:]
+    entries = bodies_ref.shape[1]
+    codes = codes_ref.shape[2]
+    tiles_tri = facet.shape[2]
+    tiles = arrived_ref.shape[0] // 8
+
+    turned = jnp.transpose(arrived_ref[...])[0:64]
+    squared = turned * turned
+    for q in range(2 * tiles):
+        at = slice(64 * q, 64 * q + 64)
+        for ref, source, i in ((px, turned, 0), (py, turned, 1), (pz, turned, 2), (rr, squared, 3)):
+            lane = 4 * q + i
+            ref[at, :] = jnp.broadcast_to(source[:, lane : lane + 1], (64, LANES))
+    for tile in range(tiles):
+        state = state_tile(arrived_ref, tile)
+        for i in range(3):
+            place[i, tile : tile + 1, :] = state[i : i + 1]
+
+    for acc in accs:
+        acc[...] = jnp.zeros_like(acc)
 
     def one_tile(entry, number):
         code = codes_ref[0, entry, number]
@@ -191,7 +194,8 @@
         parts = (fx, fy, fz, y * fz - z * fy, z * fx - x * fz, x * fy - y * fx)
         mine = jnp.zeros((1, LANES), jnp.float32)
         for i, part in enumerate(parts):
-            mine = jnp.where(lane == i, total_of(part), mine)
+            scale = time_step / (body_mass if i < 3 else body_inertia)
+            mine = jnp.where(lane == i, total_of(part) * scale, mine)
         out = out + jnp.where(owner == bodies_ref[0, entry], mine * (-stiff_wall), 0.0)
         whole = [whole[0] + fx, whole[1] + fy, whole[2] + fz]
     wrench_ref[...] = out
@@ -199,7 +203,7 @@
         force_ref[i] = stiff_wall * whole[i]
 
 
-def pair_kernel(arrived_ref, force_ref, out_ref, left, right, moved):
+def pair_kernel(arrived_ref, force_ref, out_hbm, left, right, moved, out_ref, out_sem):
     tiles = arrived_ref.shape[0] // 8
     blocks = tiles * LANES // PAIR_BLOCK
     row8 = iota((8, LANES), 0)
@@ -253,9 +257,16 @@
             )
             result = jnp.where(live, result, 0.0)
             out_ref[:, pl.ds(pl.multiple_of(tile * LANES, LANES), LANES)] = result[0:7]
+        leave(ib).start()
         return carry
 
+    def leave(ib):
+        columns = pl.ds(pl.multiple_of(ib * PAIR_BLOCK, PAIR_BLOCK), PAIR_BLOCK)
+        return pltpu.make_async_copy(out_ref.at[:, columns], out_hbm.at[:, columns], out_sem.at[ib])
+
     lax.fori_loop(0, blocks, block_of, 0)
+    for ib in range(blocks):
+        leave(ib).wait()
 
 
 def whole_vmem():
@@ -264,6 +275,10 @@
 
 def whole_smem():
     return pl.BlockSpec(memory_space=pltpu.SMEM)
+
+
+def near(x):
+    return pltpu.with_memory_space_constraint(x, pltpu.VMEM)
 
 
 def fast(sph_state, sph_dest, body_list, tile_codes, triangles):
@@ -279,7 +294,7 @@
     ]
     outgoing = pl.pallas_call(
         pack_kernel,
-        out_shape=jax.ShapeDtypeStruct((words, LANES), jnp.float32),
+        out_shape=pltpu.VMEM((words, LANES), jnp.float32),
         in_specs=[whole_vmem(), whole_vmem()],
         out_specs=whole_vmem(),
         name="pack",
@@ -290,28 +305,33 @@
     entries = body_list.shape[1]
     column = pltpu.VMEM((slots, LANES), jnp.float32)
     tiles = slots // LANES
+    facets = pl.pallas_call(
+        functools.partial(facet_kernel, sectors),
+        out_shape=pltpu.VMEM((entries, 15) + block.shape[1:], jnp.float32),
+        in_specs=[whole_smem(), pl.BlockSpec(memory_space=pltpu.HBM)] + [whole_vmem()] * (sectors - 1),
+        out_specs=whole_vmem(),
+        scratch_shapes=[pltpu.VMEM((entries,) + block.shape, jnp.float32), pltpu.SemaphoreType.DMA((entries,))],
+        name="facet",
+    )(body_list, blocks[0], *[near(other) for other in blocks[1:]])
     wrench, force = pl.pallas_call(
         functools.partial(wall_kernel, sectors, bins),
         out_shape=[
-            jax.ShapeDtypeStruct((ndevices, LANES), jnp.float32),
-            jax.ShapeDtypeStruct((3, tiles, LANES), jnp.float32),
+            pltpu.VMEM((ndevices, LANES), jnp.float32),
+            pltpu.VMEM((3, tiles, LANES), jnp.float32),
         ],
-        in_specs=[whole_smem(), whole_smem()] + [pl.BlockSpec(memory_space=pl.ANY)] * sectors + [whole_vmem()],
+        in_specs=[whole_smem(), whole_smem(), whole_vmem(), whole_vmem()],
         out_specs=[whole_vmem()] * 2,
         scratch_shapes=[
-            pltpu.VMEM((entries,) + block.shape, jnp.float32),
-            pltpu.VMEM((entries, 15) + block.shape[1:], jnp.float32),
             column,
             column,
             column,
             column,
             pltpu.VMEM((3, tiles, LANES), jnp.float32),
             pltpu.VMEM((3 * entries, tiles, LANES), jnp.float32),
-            pltpu.SemaphoreType.DMA((entries,)),
         ]
         + [column] * (3 * entries),
         name="wall",
-    )(body_list, tile_codes, *blocks, arrived)
+    )(body_list, tile_codes, near(facets), near(arrived))
     shared = lax.all_to_all(
         wrench.reshape(ndevices, 1, LANES), ("sector", "bin"), split_axis=0, concat_axis=0, tiled=True
     )
@@ -319,16 +339,17 @@
         pair_kernel,
         out_shape=jax.ShapeDtypeStruct((7, slots), jnp.float32),
         in_specs=[whole_vmem(), whole_vmem()],
-        out_specs=whole_vmem(),
+        out_specs=pl.BlockSpec(memory_space=pltpu.HBM),
         scratch_shapes=[
             pltpu.VMEM((slots, LANES), jnp.bfloat16),
             pltpu.VMEM((48, slots), jnp.bfloat16),
             pltpu.VMEM((32, slots), jnp.bfloat16),
+            pltpu.VMEM((7, slots), jnp.float32),
+            pltpu.SemaphoreType.DMA((slots // PAIR_BLOCK,)),
         ],
         name="pair",
-    )(arrived, force)
-    scaling = jnp.array([time_step / body_mass] * 3 + [time_step / body_inertia] * 3, jnp.float32)
-    kick = jnp.sum(shared[:, 0, :6], 0, keepdims=True) * scaling[None, :]
+    )(near(arrived), near(force))
+    kick = jnp.sum(shared[:, 0, :6], 0, keepdims=True)
     return new_block, kick
 
 

time: 49.6 us -> 46.9 us (0.946)
  blocking collectives: 13.7 us -> 0 us
  starting transfers between devices: 7.19 us -> 13.4 us
  waiting for transfers between devices: 0.01 us -> 5.69 us
  local copies, waits for them, and re-layouts: 1.32 us -> 0 us
  Pallas kernels: 25.7 us -> 26.3 us
    all_to_all x1 -> x0, blocking collectives: 13.7 us -> none  [fast(): lax.all_to_all(outgoing, ('sector', 'bin'), split_axis=0, concat_axis=0,...]
    all_to_all x0 -> x1, starting transfers between devices: none -> 6.3 us  [fast(): lax.all_to_all(outgoing, ('sector', 'bin'), split_axis=0, concat_axis=0,...]
    all_to_all x0 -> x1, waiting for transfers between devices: none -> 5.68 us  [fast(): lax.all_to_all(outgoing, ('sector', 'bin'), split_axis=0, concat_axis=0,...]
    pallas_call x1 -> x2, Pallas kernels: 2.91 us -> 4.58 us  [the longest x1 2.91 us: fast(): pl.pallas_call(pack_kernel, out_shape=pltpu.VMEM((words, LANES), jnp.floa...]
    unnamed x8 -> x0, local copies, waits for them, and re-layouts: 1.32 us -> none
    pallas_call x1, Pallas kernels: 9.01 us -> 8.21 us  [fast(): pl.pallas_call(pair_kernel, out_shape=jax.ShapeDtypeStruct((7, slots), jn...]
    mul x1 -> x0, other arithmetic: 0.51 us -> none  [fast(): kick = jnp.sum(shared[:, 0, :6], 0, keepdims=True) * scaling[None, :]]
    reduce_sum x1, other arithmetic: 0.05 us -> 0.56 us  [fast(): kick = jnp.sum(shared[:, 0, :6], 0, keepdims=True)]
  transfers between devices with their start and end apart: 4 -> 5, of which waited for: 0 -> 1; matrix products, arithmetic and copies ran while one was open for 0% -> 0% of each run, Pallas kernels for 24% -> 27%
where the time goes in v2:
time: 46.9 us; the launch traced here: 46.6 us
  Pallas kernels  26.3 us (56%)
  starting transfers between devices  13.4 us (29%)
  waiting for transfers between devices  5.69 us (12%)
  between operations  0.7 us (1%)
  other arithmetic  0.56 us (1%)
    pallas_call x1, Pallas kernels, fast(): pl.pallas_call(functools.partial(wall_kernel, sectors, bins), out_shape=[...  13.5 us
    pallas_call x1, Pallas kernels, fast(): pl.pallas_call(pair_kernel, out_shape=jax.ShapeDtypeStruct((7, slots), jn...  8.21 us
    all_to_all x1, starting transfers between devices, fast(): lax.all_to_all(outgoing, ('sector', 'bin'), split_axis=0, concat_axis=0,...  6.3 us
    all_to_all x1, waiting for transfers between devices, fast(): lax.all_to_all(outgoing, ('sector', 'bin'), split_axis=0, concat_axis=0,...  5.68 us
    ppermute x3, starting transfers between devices, fast(): lax.ppermute(block, 'sector', [(i, i ^ step) for i in range(sectors)])  4.57 us
    pallas_call x1, Pallas kernels, fast(): pl.pallas_call(pack_kernel, out_shape=pltpu.VMEM((words, LANES), jnp.floa...  2.91 us
    all_to_all x1, starting transfers between devices, fast(): lax.all_to_all(wrench.reshape(ndevices, 1, LANES), ('sector', 'bin'), spl...  2.48 us
    pallas_call x1, Pallas kernels, fast(): pl.pallas_call(functools.partial(facet_kernel, sectors), out_shape=pltpu....  1.67 us
  transfers between devices with their start and end apart: 5, of which 1 were waited for; matrix products, arithmetic and copies ran while one was open for 0% of the time, Pallas kernels for 27%

profile of v2, /device:TPU:0, one launch (start us, length us, event | category | flops | bytes accessed | tf_op | source)
XLA Modules:
  0.0 46.6 jit_solution(7913841928938700514)
XLA Ops:
  0.6 3.0 %collective-permute-start = (f32[9,32,128]{2,1,0:T(8,128)}, f32[9,32,128]{2,1,0:T(8,128)S(1)}, u32[]{:S(2)}, u32[]{:S(2)}) collective-permute-start(f32[9,32,128]{2,1,0:T(8,128)} %bitcast.10), channel_id=1, source_target_pairs={{0,8},{8,0},{16,24},{24,16},{1,9},{9,1},{17,25},{25,17},{2,10},{10... | collective-permute-start | bytes 442376 | tf_op jit(solution)/shard_map/ppermute | solution.py:293
  3.7 1.5 %collective-permute-start.1 = (f32[9,32,128]{2,1,0:T(8,128)}, f32[9,32,128]{2,1,0:T(8,128)S(1)}, u32[]{:S(2)}, u32[]{:S(2)}) collective-permute-start(f32[9,32,128]{2,1,0:T(8,128)} %bitcast.11), channel_id=1, source_target_pairs={{0,16},{8,24},{16,0},{24,8},{1,17},{9,25},{17,1},{25,9},{2,18},{10... | collective-permute-start | bytes 442376 | tf_op jit(solution)/shard_map/ppermute | solution.py:293
  5.2 0.0 collective-permute-start.2
  5.2 2.9 %pack.1 = f32[128,128]{1,0:T(8,128)} custom-call(s32[8,128]{1,0:T(8,128)} %bitcast.14, f32[7,1024]{1,0:T(8,128)} %state_ref.1), custom_call_target="tpu_custom_call" | custom-call | tf_op jit(solution)/shard_map/pack/pallas_call | solution.py:295
  8.1 6.3 %all-to-all-start = ((f32[32,1,512]{2,1,0:T(1,128)}), f32[32,1,512]{2,1,0:T(1,128)S(1)}, u32[]{:S(2)}, u32[]{:S(2)}) async-start(f32[32,1,512]{2,1,0:T(1,128)} %bitcast.1), calls=%async_computation | async-start | bytes 131072 | tf_op jit(solution)/shard_map/all_to_all | solution.py:303
  14.4 0.0 collective-permute-done.refs_2_
  14.4 0.0 collective-permute-done.1.refs_3_
  14.4 0.0 collective-permute-done.2.refs_4_
  14.5 1.7 %facet.1.refs_2_ = f32[2,15,32,128]{3,2,1,0:T(8,128)S(1)} custom-call(s32[1,2]{1,0:T(1,128)} %refs_0_.3, f32[9,32,128]{2,1,0:T(8,128)} %bitcast.13, f32[9,32,128]{2,1,0:T(8,128)S(1)} %collective-permute-done.refs_2_, f32[9,32,128]{2,1,0:T(8,128)S(1)} %collective-permute-done.1.refs_3_, f32[9,32,128]{2,1,0:T(8,128)S(1)} %collective-permute-done.2.refs_4_), custom_call_target="tpu_custom_call" | custom-call | tf_op jit(solution)/shard_map/facet/pallas_call | solution.py:308
  16.1 5.7 %all-to-all-done = f32[32,1,512]{2,1,0:T(1,128)S(1)} async-done(((f32[32,1,512]{2,1,0:T(1,128)}), f32[32,1,512]{2,1,0:T(1,128)S(1)}, u32[]{:S(2)}, u32[]{:S(2)}) %all-to-all-start) | async-done | bytes 65568 | tf_op jit(solution)/shard_map/all_to_all | solution.py:303
  21.8 13.5 %wall.1 = (f32[32,128]{1,0:T(8,128)}, f32[3,16,128]{2,1,0:T(8,128)S(1)}) custom-call(s32[1,2]{1,0:T(1,128)} %refs_0_.3, s32[1,2,32]{2,1,0:T(2,128)} %refs_1_.1, f32[2,15,32,128]{3,2,1,0:T(8,128)S(1)} %facet.1.refs_2_, f32[128,128]{1,0:T(8,128)S(1)} %bitcast.8), custom_call_target="tpu_custom_call" | custom-call | tf_op jit(solution)/shard_map/wall/pallas_call | solution.py:316
  35.3 2.5 %all-to-all-start.1 = ((f32[32,1,128]{2,1,0:T(1,128)}), f32[32,1,128]{2,1,0:T(1,128)S(1)}, u32[]{:S(2)}, u32[]{:S(2)}) async-start(f32[32,1,128]{2,1,0:T(1,128)} %bitcast.5), calls=%async_computation.1 | async-start | bytes 32768 | tf_op jit(solution)/shard_map/all_to_all | solution.py:335
  37.8 8.2 %pair.1 = f32[7,2048]{1,0:T(8,128)} custom-call(f32[128,128]{1,0:T(8,128)S(1)} %bitcast.9, f32[3,16,128]{2,1,0:T(8,128)S(1)} %get-tuple-element.4.force_ref), custom_call_target="tpu_custom_call" | custom-call | tf_op jit(solution)/shard_map/pair/pallas_call | solution.py:338
  46.0 0.0 all-to-all-done.1
  46.0 0.6 %slice_reduce_fusion = f32[6]{0:T(128)} fusion(f32[32,1,128]{2,1,0:T(1,128)S(1)} %all-to-all-done.1), kind=kLoop, calls=%fused_computation | loop fusion | flops 186 | bytes 792 | tf_op jit(solution)/shard_map/reduce_sum | solution.py:352
Async XLA Ops:
  0.6 13.8 %collective-permute-start = (f32[9,32,128]{2,1,0:T(8,128)}, f32[9,32,128]{2,1,0:T(8,128)S(1)}, u32[]{:S(2)}, u32[]{:S(2)}) collective-permute-start(f32[9,32,128]{2,1,0:T(8,128)} %bitcast.10), channel_id=1, source_target_pairs={{0,8},{8,0},{16,24},{24,16},{1,9},{9,1},{17,25},{25,17},{2,10},{10... | collective-permute-start | bytes 442376 | tf_op jit(solution)/shard_map/ppermute | solution.py:293
  3.7 10.8 %collective-permute-start.1 = (f32[9,32,128]{2,1,0:T(8,128)}, f32[9,32,128]{2,1,0:T(8,128)S(1)}, u32[]{:S(2)}, u32[]{:S(2)}) collective-permute-start(f32[9,32,128]{2,1,0:T(8,128)} %bitcast.11), channel_id=1, source_target_pairs={{0,16},{8,24},{16,0},{24,8},{1,17},{9,25},{17,1},{25,9},{2,18},{10... | collective-permute-start | bytes 442376 | tf_op jit(solution)/shard_map/ppermute | solution.py:293
  5.2 9.3 %collective-permute-start.2 = (f32[9,32,128]{2,1,0:T(8,128)}, f32[9,32,128]{2,1,0:T(8,128)S(1)}, u32[]{:S(2)}, u32[]{:S(2)}) collective-permute-start(f32[9,32,128]{2,1,0:T(8,128)} %bitcast.12), channel_id=1, source_target_pairs={{0,24},{8,16},{16,8},{24,0},{1,25},{9,17},{17,9},{25,1},{2,26},{10... | collective-permute-start | bytes 442376 | tf_op jit(solution)/shard_map/ppermute | solution.py:293
  8.1 13.7 %all-to-all-start = ((f32[32,1,512]{2,1,0:T(1,128)}), f32[32,1,512]{2,1,0:T(1,128)S(1)}, u32[]{:S(2)}, u32[]{:S(2)}) async-start(f32[32,1,512]{2,1,0:T(1,128)} %bitcast.1), calls=%async_computation | async-start | bytes 131072 | tf_op jit(solution)/shard_map/all_to_all | solution.py:303
  35.3 10.7 %all-to-all-start.1 = ((f32[32,1,128]{2,1,0:T(1,128)}), f32[32,1,128]{2,1,0:T(1,128)S(1)}, u32[]{:S(2)}, u32[]{:S(2)}) async-start(f32[32,1,128]{2,1,0:T(1,128)} %bitcast.5), calls=%async_computation.1 | async-start | bytes 32768 | tf_op jit(solution)/shard_map/all_to_all | solution.py:335

commit v3 on v2

--- a/solution.py
+++ b/solution.py
@@ -18,7 +18,7 @@
 LANES = 128
 PAYLOAD = ((0, 3), (1, 4), (2, 5), (6, None))
 PAIR_BLOCK = 256
-WALL_ROWS = 128
+SPREAD = 4
 
 
 def iota(shape, dim):
@@ -76,6 +76,15 @@
         out_ref[pl.ds(k, ndevices, stride=groups), :] = out[:, k * LANES : (k + 1) * LANES]
 
 
+def quotient(code, size):
+    power = size & (size - 1) == 0
+    return lax.shift_right_logical(code, size.bit_length() - 1) if power else lax.div(code, size)
+
+
+def remainder(code, size):
+    return code & (size - 1) if size & (size - 1) == 0 else lax.rem(code, size)
+
+
 def total_of(x):
     return jnp.sum(jnp.sum(x, 0, keepdims=True), 1, keepdims=True)
 
@@ -122,52 +131,67 @@
             facet[entry, 12 + i] = (d11 * two[i] - d12 * one[i]) * inverse
 
 
+def sphere_side(state, row8):
+    square = state * state
+    level = square[3:4] - (square[0:1] + square[1:2] + square[2:3])
+    other = jnp.where(state[3:4] > 0.0, level, -3.0e38)
+    return level, jnp.where(
+        row8 < 4, state, jnp.where(row8 == 4, 1.0, jnp.where(row8 == 5, other, jnp.where(row8 == 6, square[3:4], 0.0)))
+    )
+
+
 def wall_kernel(sectors, bins, *refs):
-    bodies_ref, codes_ref, facet, arrived_ref, wrench_ref, force_ref, px, py, pz, rr, place, gathered = refs[:12]
-    accs = refs[12:]
+    bodies_ref, codes_ref, facet, arrived_ref, wrench_ref, force_ref, left = refs[:7]
+    spread, place, gathered = refs[7:10]
+    accs = refs[10:]
     entries = bodies_ref.shape[1]
     codes = codes_ref.shape[2]
     tiles_tri = facet.shape[2]
     tiles = arrived_ref.shape[0] // 8
-
-    turned = jnp.transpose(arrived_ref[...])[0:64]
-    squared = turned * turned
-    for q in range(2 * tiles):
-        at = slice(64 * q, 64 * q + 64)
-        for ref, source, i in ((px, turned, 0), (py, turned, 1), (pz, turned, 2), (rr, squared, 3)):
-            lane = 4 * q + i
-            ref[at, :] = jnp.broadcast_to(source[:, lane : lane + 1], (64, LANES))
+    row8 = iota((8, LANES), 0)
+
+    wanted = iota((48, 4 * LANES), 1) // LANES
+    wanted = jnp.where(wanted == 3, 6, wanted)
+    row = iota((48, 4 * LANES), 0)
+    select = (row % 8 == wanted) & ((row // 8 == 0) | (row // 8 == 1) | (row // 8 == 3))
+    select = select.astype(jnp.float32).astype(jnp.bfloat16)
     for tile in range(tiles):
+        at = slice(tile * LANES, (tile + 1) * LANES)
         state = state_tile(arrived_ref, tile)
+        jh, jm, jl = split3(sphere_side(state, row8)[1])
+        left[at, 0:48] = jnp.transpose(jnp.concatenate([jh, jm, jh, jl, jh, jm], 0)).astype(jnp.bfloat16)
         for i in range(3):
             place[i, tile : tile + 1, :] = state[i : i + 1]
-
+    for group in range(tiles // SPREAD):
+        at = slice(group * SPREAD * LANES, (group + 1) * SPREAD * LANES)
+        wide = dot(left[at, 0:48], select)
+        for i in range(4):
+            spread[i, at, :] = wide[:, i * LANES : (i + 1) * LANES]
     for acc in accs:
         acc[...] = jnp.zeros_like(acc)
 
     def one_tile(entry, number):
         code = codes_ref[0, entry, number]
-        first = pl.multiple_of(code // tiles_tri * LANES, LANES)
-        facet_tile = code % tiles_tri
+        first = pl.multiple_of(quotient(code, tiles_tri) * LANES, LANES)
+        facet_tile = remainder(code, tiles_tri)
         f = [facet[entry, i, pl.ds(facet_tile, 1), :] for i in range(15)]
-        for part in range(LANES // WALL_ROWS):
-            at = pl.ds(pl.multiple_of(first + part * WALL_ROWS, WALL_ROWS), WALL_ROWS)
-            dx, dy, dz = px[at, :] - f[0], py[at, :] - f[1], pz[at, :] - f[2]
-            beta = dx * f[9] + dy * f[10] + dz * f[11]
-            gamma = dx * f[12] + dy * f[13] + dz * f[14]
-            alpha = jnp.maximum(1.0 - beta - gamma, 0.0)
-            beta = jnp.maximum(beta, 0.0)
-            gamma = jnp.maximum(gamma, 0.0)
-            scale = 1.0 / (alpha + beta + gamma)
-            beta = beta * scale
-            gamma = gamma * scale
-            ox = dx - beta * f[3] - gamma * f[6]
-            oy = dy - beta * f[4] - gamma * f[7]
-            oz = dz - beta * f[5] - gamma * f[8]
-            deep = jnp.maximum(rr[at, :] - (ox * ox + oy * oy + oz * oz), 0.0)
-            accs[3 * entry][at, :] += deep * ox
-            accs[3 * entry + 1][at, :] += deep * oy
-            accs[3 * entry + 2][at, :] += deep * oz
+        at = pl.ds(first, LANES)
+        dx, dy, dz = spread[0, at, :] - f[0], spread[1, at, :] - f[1], spread[2, at, :] - f[2]
+        beta = dx * f[9] + dy * f[10] + dz * f[11]
+        gamma = dx * f[12] + dy * f[13] + dz * f[14]
+        alpha = jnp.maximum(1.0 - beta - gamma, 0.0)
+        beta = jnp.maximum(beta, 0.0)
+        gamma = jnp.maximum(gamma, 0.0)
+        scale = 1.0 / (alpha + beta + gamma)
+        beta = beta * scale
+        gamma = gamma * scale
+        ox = dx - beta * f[3] - gamma * f[6]
+        oy = dy - beta * f[4] - gamma * f[7]
+        oz = dz - beta * f[5] - gamma * f[8]
+        deep = jnp.maximum(spread[3, at, :] - (ox * ox + oy * oy + oz * oz), 0.0)
+        accs[3 * entry][at, :] += deep * ox
+        accs[3 * entry + 1][at, :] += deep * oy
+        accs[3 * entry + 2][at, :] += deep * oz
 
     def step(number, carry):
         for entry in range(entries):
@@ -176,14 +200,19 @@
 
     lax.fori_loop(0, codes, step, 0)
 
+    ones = jnp.ones((16, 2 * LANES), jnp.bfloat16)
+
     def gather(tile, carry):
         at = pl.ds(pl.multiple_of(tile * LANES, LANES), LANES)
         for which in range(3 * entries):
-            row = jnp.sum(jnp.transpose(accs[which][at, :]), 0, keepdims=True)
-            gathered[which, pl.ds(tile, 1), :] = row
+            value = accs[which][at, :]
+            high = value.astype(jnp.bfloat16)
+            low = (value - high.astype(jnp.float32)).astype(jnp.bfloat16)
+            row = dot(ones, jnp.concatenate([high, low], 1), ((1,), (1,)))
+            gathered[which, pl.ds(tile, 1), :] = row[0:1]
         return carry
 
-    lax.fori_loop(0, tiles, gather, 0)
+    lax.fori_loop(0, tiles, gather, 0, unroll=2)
     x, y, z = place[0], place[1], place[2]
     owner = iota((sectors * bins, LANES), 0) // bins
     lane = iota((1, LANES), 1)
@@ -203,22 +232,17 @@
         force_ref[i] = stiff_wall * whole[i]
 
 
-def pair_kernel(arrived_ref, force_ref, out_hbm, left, right, moved, out_ref, out_sem):
+def pair_kernel(arrived_ref, force_ref, left, out_hbm, right, moved, out_ref, out_sem):
     tiles = arrived_ref.shape[0] // 8
     blocks = tiles * LANES // PAIR_BLOCK
     row8 = iota((8, LANES), 0)
     for tile in range(tiles):
         at = slice(tile * LANES, (tile + 1) * LANES)
         state = state_tile(arrived_ref, tile)
-        square = state * state
-        level = square[3:4] - (square[0:1] + square[1:2] + square[2:3])
-        other = jnp.where(state[3:4] > 0.0, level, -3.0e38)
+        level = sphere_side(state, row8)[0]
         i_side = jnp.where(row8 < 4, 2.0 * state, jnp.where(row8 == 4, level, jnp.where(row8 == 5, 1.0, 0.0)))
-        j_side = jnp.where(row8 < 4, state, jnp.where(row8 == 4, 1.0, jnp.where(row8 == 5, other, 0.0)))
         ih, im, il = split3(i_side)
-        jh, jm, jl = split3(j_side)
         right[:, at] = jnp.concatenate([ih, ih, im, ih, il, im], 0).astype(jnp.bfloat16)
-        left[at, 0:48] = jnp.transpose(jnp.concatenate([jh, jm, jh, jl, jh, jm], 0)).astype(jnp.bfloat16)
         value = jnp.where(row8 == 3, 1.0, state)
         moved[:, at] = jnp.concatenate(list(split3(value)) + [jnp.zeros((8, LANES), jnp.float32)], 0).astype(
             jnp.bfloat16
@@ -313,19 +337,17 @@
         scratch_shapes=[pltpu.VMEM((entries,) + block.shape, jnp.float32), pltpu.SemaphoreType.DMA((entries,))],
         name="facet",
     )(body_list, blocks[0], *[near(other) for other in blocks[1:]])
-    wrench, force = pl.pallas_call(
+    wrench, force, left = pl.pallas_call(
         functools.partial(wall_kernel, sectors, bins),
         out_shape=[
             pltpu.VMEM((ndevices, LANES), jnp.float32),
             pltpu.VMEM((3, tiles, LANES), jnp.float32),
+            pltpu.VMEM((slots, LANES), jnp.bfloat16),
         ],
-        in_specs=[whole_smem(), whole_smem(), whole_vmem(), whole_vmem()],
-        out_specs=[whole_vmem()] * 2,
+        in_specs=[whole_smem(), whole_smem()] + [whole_vmem()] * 2,
+        out_specs=[whole_vmem()] * 3,
         scratch_shapes=[
-            column,
-            column,
-            column,
-            column,
+            pltpu.VMEM((4, slots, LANES), jnp.float32),
             pltpu.VMEM((3, tiles, LANES), jnp.float32),
             pltpu.VMEM((3 * entries, tiles, LANES), jnp.float32),
         ]
@@ -338,17 +360,16 @@
     new_block = pl.pallas_call(
         pair_kernel,
         out_shape=jax.ShapeDtypeStruct((7, slots), jnp.float32),
-        in_specs=[whole_vmem(), whole_vmem()],
+        in_specs=[whole_vmem()] * 3,
         out_specs=pl.BlockSpec(memory_space=pltpu.HBM),
         scratch_shapes=[
-            pltpu.VMEM((slots, LANES), jnp.bfloat16),
             pltpu.VMEM((48, slots), jnp.bfloat16),
             pltpu.VMEM((32, slots), jnp.bfloat16),
             pltpu.VMEM((7, slots), jnp.float32),
             pltpu.SemaphoreType.DMA((slots // PAIR_BLOCK,)),
         ],
         name="pair",
-    )(near(arrived), near(force))
+    )(near(arrived), near(force), near(left))
     kick = jnp.sum(shared[:, 0, :6], 0, keepdims=True)
     return new_block, kick
 

time: 46.9 us -> 45.7 us (0.974)
  Pallas kernels: 26.3 us -> 24.6 us
  waiting for transfers between devices: 5.69 us -> 6.19 us
    pallas_call x1, Pallas kernels: 13.5 us -> 12.9 us  [fast(): pl.pallas_call(functools.partial(wall_kernel, sectors, bins), out_shape=[...]
    pallas_call x1, Pallas kernels: 8.21 us -> 7.63 us  [fast(): pl.pallas_call(pair_kernel, out_shape=jax.ShapeDtypeStruct((7, slots), jn...]
    all_to_all x1, waiting for transfers between devices: 5.68 us -> 6.18 us  [fast(): lax.all_to_all(outgoing, ('sector', 'bin'), split_axis=0, concat_axis=0,...]
    pallas_call x1, Pallas kernels: 1.67 us -> 1.17 us  [fast(): pl.pallas_call(functools.partial(facet_kernel, sectors), out_shape=pltpu....]
  transfers between devices with their start and end apart: 5 -> 5, of which waited for: 1 -> 1; matrix products, arithmetic and copies ran while one was open for 0% -> 0% of each run, Pallas kernels for 27% -> 26%
where the time goes in v3:
time: 45.7 us; the launch traced here: 45.4 us
  Pallas kernels  24.6 us (54%)
  starting transfers between devices  13.4 us (29%)
  waiting for transfers between devices  6.19 us (14%)
  between operations  0.7 us (2%)
  other arithmetic  0.56 us (1%)
    pallas_call x1, Pallas kernels, fast(): pl.pallas_call(functools.partial(wall_kernel, sectors, bins), out_shape=[...  12.9 us
    pallas_call x1, Pallas kernels, fast(): pl.pallas_call(pair_kernel, out_shape=jax.ShapeDtypeStruct((7, slots), jn...  7.63 us
    all_to_all x1, starting transfers between devices, fast(): lax.all_to_all(outgoing, ('sector', 'bin'), split_axis=0, concat_axis=0,...  6.25 us
    all_to_all x1, waiting for transfers between devices, fast(): lax.all_to_all(outgoing, ('sector', 'bin'), split_axis=0, concat_axis=0,...  6.18 us
    ppermute x3, starting transfers between devices, fast(): lax.ppermute(block, 'sector', [(i, i ^ step) for i in range(sectors)])  4.63 us
    pallas_call x1, Pallas kernels, fast(): pl.pallas_call(pack_kernel, out_shape=pltpu.VMEM((words, LANES), jnp.floa...  2.91 us
    all_to_all x1, starting transfers between devices, fast(): lax.all_to_all(wrench.reshape(ndevices, 1, LANES), ('sector', 'bin'), spl...  2.48 us
    pallas_call x1, Pallas kernels, fast(): pl.pallas_call(functools.partial(facet_kernel, sectors), out_shape=pltpu....  1.17 us
  transfers between devices with their start and end apart: 5, of which 1 were waited for; matrix products, arithmetic and copies ran while one was open for 0% of the time, Pallas kernels for 26%

profile of v3, /device:TPU:0, one launch (start us, length us, event | category | flops | bytes accessed | tf_op | source)
XLA Modules:
  0.0 45.4 jit_solution(7625621235642324391)
XLA Ops:
  0.6 4.0 %collective-permute-start.2 = (f32[9,32,128]{2,1,0:T(8,128)}, f32[9,32,128]{2,1,0:T(8,128)S(1)}, u32[]{:S(2)}, u32[]{:S(2)}) collective-permute-start(f32[9,32,128]{2,1,0:T(8,128)} %bitcast.10), channel_id=1, source_target_pairs={{0,24},{8,16},{16,8},{24,0},{1,25},{9,17},{17,9},{25,1},{2,26},{10... | collective-permute-start | bytes 442376 | tf_op jit(solution)/shard_map/ppermute | solution.py:317
  4.6 0.5 %collective-permute-start.1 = (f32[9,32,128]{2,1,0:T(8,128)}, f32[9,32,128]{2,1,0:T(8,128)S(1)}, u32[]{:S(2)}, u32[]{:S(2)}) collective-permute-start(f32[9,32,128]{2,1,0:T(8,128)} %bitcast.11), channel_id=1, source_target_pairs={{0,16},{8,24},{16,0},{24,8},{1,17},{9,25},{17,1},{25,9},{2,18},{10... | collective-permute-start | bytes 442376 | tf_op jit(solution)/shard_map/ppermute | solution.py:317
  5.1 0.1 collective-permute-start
  5.3 2.9 %pack.1 = f32[128,128]{1,0:T(8,128)} custom-call(s32[8,128]{1,0:T(8,128)} %bitcast.14, f32[7,1024]{1,0:T(8,128)} %state_ref.1), custom_call_target="tpu_custom_call" | custom-call | tf_op jit(solution)/shard_map/pack/pallas_call | solution.py:319
  8.2 6.2 %all-to-all-start = ((f32[32,1,512]{2,1,0:T(1,128)}), f32[32,1,512]{2,1,0:T(1,128)S(1)}, u32[]{:S(2)}, u32[]{:S(2)}) async-start(f32[32,1,512]{2,1,0:T(1,128)} %bitcast.1), calls=%async_computation | async-start | bytes 131072 | tf_op jit(solution)/shard_map/all_to_all | solution.py:327
  14.4 0.0 collective-permute-done.2.refs_4_
  14.4 0.0 collective-permute-done.1.refs_3_
  14.4 0.0 collective-permute-done.refs_2_
  14.5 1.2 %facet.1.refs_2_ = f32[2,15,32,128]{3,2,1,0:T(8,128)S(1)} custom-call(s32[1,2]{1,0:T(1,128)} %refs_0_.3, f32[9,32,128]{2,1,0:T(8,128)} %bitcast.13, f32[9,32,128]{2,1,0:T(8,128)S(1)} %collective-permute-done.refs_2_, f32[9,32,128]{2,1,0:T(8,128)S(1)} %collective-permute-done.1.refs_3_, f32[9,32,128]{2,1,0:T(8,128)S(1)} %collective-permute-done.2.refs_4_), custom_call_target="tpu_custom_call" | custom-call | tf_op jit(solution)/shard_map/facet/pallas_call | solution.py:332
  15.6 6.2 %all-to-all-done = f32[32,1,512]{2,1,0:T(1,128)S(1)} async-done(((f32[32,1,512]{2,1,0:T(1,128)}), f32[32,1,512]{2,1,0:T(1,128)S(1)}, u32[]{:S(2)}, u32[]{:S(2)}) %all-to-all-start) | async-done | bytes 65568 | tf_op jit(solution)/shard_map/all_to_all | solution.py:327
  21.8 12.9 %wall.1 = (f32[32,128]{1,0:T(8,128)}, f32[3,16,128]{2,1,0:T(8,128)S(1)}, bf16[2048,128]{1,0:T(8,128)(2,1)S(1)}) custom-call(s32[1,2]{1,0:T(1,128)} %refs_0_.3, s32[1,2,32]{2,1,0:T(2,128)} %refs_1_.1, f32[2,15,32,128]{3,2,1,0:T(8,128)S(1)} %facet.1.refs_2_, f32[128,128]{1,0:T(8,128)S(1)} %bitcast.8), custom_call_target="tpu_custom_call" | custom-call | tf_op jit(solution)/shard_map/wall/pallas_call | solution.py:340
  34.7 2.5 %all-to-all-start.1 = ((f32[32,1,128]{2,1,0:T(1,128)}), f32[32,1,128]{2,1,0:T(1,128)S(1)}, u32[]{:S(2)}, u32[]{:S(2)}) async-start(f32[32,1,128]{2,1,0:T(1,128)} %bitcast.5), calls=%async_computation.1 | async-start | bytes 32768 | tf_op jit(solution)/shard_map/all_to_all | solution.py:357
  37.2 7.6 %pair.1 = f32[7,2048]{1,0:T(8,128)} custom-call(f32[128,128]{1,0:T(8,128)S(1)} %bitcast.9, f32[3,16,128]{2,1,0:T(8,128)S(1)} %get-tuple-element.5.force_ref, bf16[2048,128]{1,0:T(8,128)(2,1)S(1)} %get-tuple-element.6.left), custom_call_target="tpu_custom_call" | custom-call | tf_op jit(solution)/shard_map/pair/pallas_call | solution.py:360
  44.8 0.0 all-to-all-done.1
  44.8 0.6 %slice_reduce_fusion = f32[6]{0:T(128)} fusion(f32[32,1,128]{2,1,0:T(1,128)S(1)} %all-to-all-done.1), kind=kLoop, calls=%fused_computation | loop fusion | flops 186 | bytes 792 | tf_op jit(solution)/shard_map/reduce_sum | solution.py:373
Async XLA Ops:
  0.6 13.8 %collective-permute-start.2 = (f32[9,32,128]{2,1,0:T(8,128)}, f32[9,32,128]{2,1,0:T(8,128)S(1)}, u32[]{:S(2)}, u32[]{:S(2)}) collective-permute-start(f32[9,32,128]{2,1,0:T(8,128)} %bitcast.10), channel_id=1, source_target_pairs={{0,24},{8,16},{16,8},{24,0},{1,25},{9,17},{17,9},{25,1},{2,26},{10... | collective-permute-start | bytes 442376 | tf_op jit(solution)/shard_map/ppermute | solution.py:317
  4.6 9.8 %collective-permute-start.1 = (f32[9,32,128]{2,1,0:T(8,128)}, f32[9,32,128]{2,1,0:T(8,128)S(1)}, u32[]{:S(2)}, u32[]{:S(2)}) collective-permute-start(f32[9,32,128]{2,1,0:T(8,128)} %bitcast.11), channel_id=1, source_target_pairs={{0,16},{8,24},{16,0},{24,8},{1,17},{9,25},{17,1},{25,9},{2,18},{10... | collective-permute-start | bytes 442376 | tf_op jit(solution)/shard_map/ppermute | solution.py:317
  5.1 9.3 %collective-permute-start = (f32[9,32,128]{2,1,0:T(8,128)}, f32[9,32,128]{2,1,0:T(8,128)S(1)}, u32[]{:S(2)}, u32[]{:S(2)}) collective-permute-start(f32[9,32,128]{2,1,0:T(8,128)} %bitcast.12), channel_id=1, source_target_pairs={{0,8},{8,0},{16,24},{24,16},{1,9},{9,1},{17,25},{25,17},{2,10},{10... | collective-permute-start | bytes 442376 | tf_op jit(solution)/shard_map/ppermute | solution.py:317
  8.2 13.6 %all-to-all-start = ((f32[32,1,512]{2,1,0:T(1,128)}), f32[32,1,512]{2,1,0:T(1,128)S(1)}, u32[]{:S(2)}, u32[]{:S(2)}) async-start(f32[32,1,512]{2,1,0:T(1,128)} %bitcast.1), calls=%async_computation | async-start | bytes 131072 | tf_op jit(solution)/shard_map/all_to_all | solution.py:327
  34.7 10.1 %all-to-all-start.1 = ((f32[32,1,128]{2,1,0:T(1,128)}), f32[32,1,128]{2,1,0:T(1,128)S(1)}, u32[]{:S(2)}, u32[]{:S(2)}) async-start(f32[32,1,128]{2,1,0:T(1,128)} %bitcast.5), calls=%async_computation.1 | async-start | bytes 32768 | tf_op jit(solution)/shard_map/all_to_all | solution.py:357

commit v4 on v3

--- a/solution.py
+++ b/solution.py
@@ -58,22 +58,29 @@
     rank_row = jnp.concatenate([ranks[b : b + 1] for b in range(blocks)], 1)
     dest_row = jnp.concatenate([dest[b : b + 1] for b in range(blocks)], 1)
     leaving = blocks * LANES
-    chosen = rank_row == iota((capacity, leaving), 0).astype(jnp.float32)
-    to_dest = (dest_row == iota((ndevices, leaving), 0)).astype(jnp.float32).astype(jnp.bfloat16)
-    out = None
-    for part in split3(state_ref[...]):
-        rows = []
-        for pair in PAYLOAD:
-            for source in pair:
-                if source is None:
-                    rows.append(jnp.zeros((capacity, leaving), jnp.bfloat16))
-                else:
-                    rows.append(jnp.where(chosen, part[source : source + 1], 0.0).astype(jnp.bfloat16))
-        piece = dot(to_dest, jnp.concatenate(rows, 0), ((1,), (1,)))
-        out = piece if out is None else out + piece
+    chosen = dest_row == iota((ndevices, leaving), 0)
+    slot = (iota((LANES, leaving), 0) % capacity).astype(jnp.float32)
+    at_rank = (rank_row == slot).astype(jnp.float32).astype(jnp.bfloat16)
     groups = len(PAYLOAD)
-    for k in range(groups):
-        out_ref[pl.ds(k, ndevices, stride=groups), :] = out[:, k * LANES : (k + 1) * LANES]
+    sources = [pair[half] for half in range(2) for pair in PAYLOAD if pair[half] is not None]
+    rows = [
+        jnp.where(chosen, part[source : source + 1], 0.0).astype(jnp.bfloat16)
+        for part in split3(state_ref[...])
+        for source in sources
+    ]
+    pieces = dot(jnp.concatenate(rows, 0), at_rank, ((1,), (1,)))
+    height = len(sources) * ndevices
+    out = (pieces[:height] + pieces[height : 2 * height]) + pieces[2 * height :]
+    low = iota((ndevices, LANES), 1) < capacity
+    for k, pair in enumerate(PAYLOAD):
+        halves = []
+        for source in pair:
+            if source is None:
+                halves.append(jnp.zeros((ndevices, LANES), jnp.float32))
+            else:
+                place = sources.index(source) * ndevices
+                halves.append(out[place : place + ndevices])
+        out_ref[pl.ds(k, ndevices, stride=groups), :] = jnp.where(low, halves[0], halves[1])
 
 
 def quotient(code, size):
@@ -313,9 +320,6 @@
     slots = 2 * leaving
     words = 8 * slots // LANES
     block = triangles.reshape(triangles.shape[0], -1, LANES)
-    blocks = [block] + [
-        lax.ppermute(block, "sector", [(i, i ^ step) for i in range(sectors)]) for step in range(1, sectors)
-    ]
     outgoing = pl.pallas_call(
         pack_kernel,
         out_shape=pltpu.VMEM((words, LANES), jnp.float32),
@@ -323,6 +327,9 @@
         out_specs=whole_vmem(),
         name="pack",
     )(sph_dest.reshape(-1, LANES), sph_state)
+    blocks = [block] + [
+        lax.ppermute(block, "sector", [(i, i ^ step) for i in range(sectors)]) for step in range(1, sectors)
+    ]
     outgoing = outgoing.reshape(ndevices, 1, words * LANES // ndevices)
     arrived = lax.all_to_all(outgoing, ("sector", "bin"), split_axis=0, concat_axis=0, tiled=True)
     arrived = arrived.reshape(words, LANES)

time: 45.7 us -> 45.3 us (level)
  waiting for transfers between devices: 6.19 us -> 5.51 us
    all_to_all x1, waiting for transfers between devices: 6.18 us -> 5.5 us  [fast(): lax.all_to_all(outgoing, ('sector', 'bin'), split_axis=0, concat_axis=0,...]
    pallas_call x1, Pallas kernels: 1.17 us -> 1.84 us  [fast(): pl.pallas_call(functools.partial(facet_kernel, sectors), out_shape=pltpu....]
  transfers between devices with their start and end apart: 5 -> 5, of which waited for: 1 -> 1; matrix products, arithmetic and copies ran while one was open for 0% -> 0% of each run, Pallas kernels for 26% -> 27%
where the time goes in v4:
time: 45.3 us; the launch traced here: 45 us
  Pallas kernels  24.9 us (55%)
  starting transfers between devices  13.4 us (30%)
  waiting for transfers between devices  5.51 us (12%)
  between operations  0.7 us (2%)
  other arithmetic  0.56 us (1%)
    pallas_call x1, Pallas kernels, fast(): pl.pallas_call(functools.partial(wall_kernel, sectors, bins), out_shape=[...  12.9 us
    pallas_call x1, Pallas kernels, fast(): pl.pallas_call(pair_kernel, out_shape=jax.ShapeDtypeStruct((7, slots), jn...  7.63 us
    all_to_all x1, starting transfers between devices, fast(): lax.all_to_all(outgoing, ('sector', 'bin'), split_axis=0, concat_axis=0,...  6.25 us
    all_to_all x1, waiting for transfers between devices, fast(): lax.all_to_all(outgoing, ('sector', 'bin'), split_axis=0, concat_axis=0,...  5.5 us
    ppermute x3, starting transfers between devices, fast(): lax.ppermute(block, 'sector', [(i, i ^ step) for i in range(sectors)])  4.63 us
    pallas_call x1, Pallas kernels, fast(): pl.pallas_call(pack_kernel, out_shape=pltpu.VMEM((words, LANES), jnp.floa...  2.54 us
    all_to_all x1, starting transfers between devices, fast(): lax.all_to_all(wrench.reshape(ndevices, 1, LANES), ('sector', 'bin'), spl...  2.48 us
    pallas_call x1, Pallas kernels, fast(): pl.pallas_call(functools.partial(facet_kernel, sectors), out_shape=pltpu....  1.84 us
  transfers between devices with their start and end apart: 5, of which 1 were waited for; matrix products, arithmetic and copies ran while one was open for 0% of the time, Pallas kernels for 27%

profile of v4, /device:TPU:0, one launch (start us, length us, event | category | flops | bytes accessed | tf_op | source)
XLA Modules:
  0.0 45.0 jit_solution(12997450325242475000)
XLA Ops:
  0.6 4.0 %collective-permute-start.2 = (f32[9,32,128]{2,1,0:T(8,128)}, f32[9,32,128]{2,1,0:T(8,128)S(1)}, u32[]{:S(2)}, u32[]{:S(2)}) collective-permute-start(f32[9,32,128]{2,1,0:T(8,128)} %bitcast.10), channel_id=1, source_target_pairs={{0,24},{8,16},{16,8},{24,0},{1,25},{9,17},{17,9},{25,1},{2,26},{10... | collective-permute-start | bytes 442376 | tf_op jit(solution)/shard_map/ppermute | solution.py:331
  4.6 0.5 %collective-permute-start.1 = (f32[9,32,128]{2,1,0:T(8,128)}, f32[9,32,128]{2,1,0:T(8,128)S(1)}, u32[]{:S(2)}, u32[]{:S(2)}) collective-permute-start(f32[9,32,128]{2,1,0:T(8,128)} %bitcast.11), channel_id=1, source_target_pairs={{0,16},{8,24},{16,0},{24,8},{1,17},{9,25},{17,1},{25,9},{2,18},{10... | collective-permute-start | bytes 442376 | tf_op jit(solution)/shard_map/ppermute | solution.py:331
  5.1 0.1 collective-permute-start
  5.3 2.5 %pack.1 = f32[128,128]{1,0:T(8,128)} custom-call(s32[8,128]{1,0:T(8,128)} %bitcast.14, f32[7,1024]{1,0:T(8,128)} %state_ref.1), custom_call_target="tpu_custom_call" | custom-call | tf_op jit(solution)/shard_map/pack/pallas_call | solution.py:323
  7.8 6.2 %all-to-all-start = ((f32[32,1,512]{2,1,0:T(1,128)}), f32[32,1,512]{2,1,0:T(1,128)S(1)}, u32[]{:S(2)}, u32[]{:S(2)}) async-start(f32[32,1,512]{2,1,0:T(1,128)} %bitcast.1), calls=%async_computation | async-start | bytes 131072 | tf_op jit(solution)/shard_map/all_to_all | solution.py:334
  14.1 0.0 collective-permute-done.2.refs_4_
  14.1 0.0 collective-permute-done.1.refs_3_
  14.1 0.0 collective-permute-done.refs_2_
  14.1 1.8 %facet.1.refs_2_ = f32[2,15,32,128]{3,2,1,0:T(8,128)S(1)} custom-call(s32[1,2]{1,0:T(1,128)} %refs_0_.3, f32[9,32,128]{2,1,0:T(8,128)} %bitcast.13, f32[9,32,128]{2,1,0:T(8,128)S(1)} %collective-permute-done.refs_2_, f32[9,32,128]{2,1,0:T(8,128)S(1)} %collective-permute-done.1.refs_3_, f32[9,32,128]{2,1,0:T(8,128)S(1)} %collective-permute-done.2.refs_4_), custom_call_target="tpu_custom_call" | custom-call | tf_op jit(solution)/shard_map/facet/pallas_call | solution.py:339
  15.9 5.5 %all-to-all-done = f32[32,1,512]{2,1,0:T(1,128)S(1)} async-done(((f32[32,1,512]{2,1,0:T(1,128)}), f32[32,1,512]{2,1,0:T(1,128)S(1)}, u32[]{:S(2)}, u32[]{:S(2)}) %all-to-all-start) | async-done | bytes 65568 | tf_op jit(solution)/shard_map/all_to_all | solution.py:334
  21.4 12.9 %wall.1 = (f32[32,128]{1,0:T(8,128)}, f32[3,16,128]{2,1,0:T(8,128)S(1)}, bf16[2048,128]{1,0:T(8,128)(2,1)S(1)}) custom-call(s32[1,2]{1,0:T(1,128)} %refs_0_.3, s32[1,2,32]{2,1,0:T(2,128)} %refs_1_.1, f32[2,15,32,128]{3,2,1,0:T(8,128)S(1)} %facet.1.refs_2_, f32[128,128]{1,0:T(8,128)S(1)} %bitcast.8), custom_call_target="tpu_custom_call" | custom-call | tf_op jit(solution)/shard_map/wall/pallas_call | solution.py:347
  34.3 2.5 %all-to-all-start.1 = ((f32[32,1,128]{2,1,0:T(1,128)}), f32[32,1,128]{2,1,0:T(1,128)S(1)}, u32[]{:S(2)}, u32[]{:S(2)}) async-start(f32[32,1,128]{2,1,0:T(1,128)} %bitcast.5), calls=%async_computation.1 | async-start | bytes 32768 | tf_op jit(solution)/shard_map/all_to_all | solution.py:364
  36.8 7.6 %pair.1 = f32[7,2048]{1,0:T(8,128)} custom-call(f32[128,128]{1,0:T(8,128)S(1)} %bitcast.9, f32[3,16,128]{2,1,0:T(8,128)S(1)} %get-tuple-element.5.force_ref, bf16[2048,128]{1,0:T(8,128)(2,1)S(1)} %get-tuple-element.6.left), custom_call_target="tpu_custom_call" | custom-call | tf_op jit(solution)/shard_map/pair/pallas_call | solution.py:367
  44.4 0.0 all-to-all-done.1
  44.5 0.6 %slice_reduce_fusion = f32[6]{0:T(128)} fusion(f32[32,1,128]{2,1,0:T(1,128)S(1)} %all-to-all-done.1), kind=kLoop, calls=%fused_computation | loop fusion | flops 186 | bytes 792 | tf_op jit(solution)/shard_map/reduce_sum | solution.py:380
Async XLA Ops:
  0.6 13.4 %collective-permute-start.2 = (f32[9,32,128]{2,1,0:T(8,128)}, f32[9,32,128]{2,1,0:T(8,128)S(1)}, u32[]{:S(2)}, u32[]{:S(2)}) collective-permute-start(f32[9,32,128]{2,1,0:T(8,128)} %bitcast.10), channel_id=1, source_target_pairs={{0,24},{8,16},{16,8},{24,0},{1,25},{9,17},{17,9},{25,1},{2,26},{10... | collective-permute-start | bytes 442376 | tf_op jit(solution)/shard_map/ppermute | solution.py:331
  4.6 9.5 %collective-permute-start.1 = (f32[9,32,128]{2,1,0:T(8,128)}, f32[9,32,128]{2,1,0:T(8,128)S(1)}, u32[]{:S(2)}, u32[]{:S(2)}) collective-permute-start(f32[9,32,128]{2,1,0:T(8,128)} %bitcast.11), channel_id=1, source_target_pairs={{0,16},{8,24},{16,0},{24,8},{1,17},{9,25},{17,1},{25,9},{2,18},{10... | collective-permute-start | bytes 442376 | tf_op jit(solution)/shard_map/ppermute | solution.py:331
  5.1 9.0 %collective-permute-start = (f32[9,32,128]{2,1,0:T(8,128)}, f32[9,32,128]{2,1,0:T(8,128)S(1)}, u32[]{:S(2)}, u32[]{:S(2)}) collective-permute-start(f32[9,32,128]{2,1,0:T(8,128)} %bitcast.12), channel_id=1, source_target_pairs={{0,8},{8,0},{16,24},{24,16},{1,9},{9,1},{17,25},{25,17},{2,10},{10... | collective-permute-start | bytes 442376 | tf_op jit(solution)/shard_map/ppermute | solution.py:331
  7.8 13.6 %all-to-all-start = ((f32[32,1,512]{2,1,0:T(1,128)}), f32[32,1,512]{2,1,0:T(1,128)S(1)}, u32[]{:S(2)}, u32[]{:S(2)}) async-start(f32[32,1,512]{2,1,0:T(1,128)} %bitcast.1), calls=%async_computation | async-start | bytes 131072 | tf_op jit(solution)/shard_map/all_to_all | solution.py:334
  34.3 10.1 %all-to-all-start.1 = ((f32[32,1,128]{2,1,0:T(1,128)}), f32[32,1,128]{2,1,0:T(1,128)S(1)}, u32[]{:S(2)}, u32[]{:S(2)}) async-start(f32[32,1,128]{2,1,0:T(1,128)} %bitcast.5), calls=%async_computation.1 | async-start | bytes 32768 | tf_op jit(solution)/shard_map/all_to_all | solution.py:364

commit v5 on v4

--- a/solution.py
+++ b/solution.py
@@ -17,7 +17,7 @@
 
 LANES = 128
 PAYLOAD = ((0, 3), (1, 4), (2, 5), (6, None))
-PAIR_BLOCK = 256
+PAIR_BLOCK = 512
 SPREAD = 4
 
 
@@ -213,13 +213,16 @@
         at = pl.ds(pl.multiple_of(tile * LANES, LANES), LANES)
         for which in range(3 * entries):
             value = accs[which][at, :]
-            high = value.astype(jnp.bfloat16)
-            low = (value - high.astype(jnp.float32)).astype(jnp.bfloat16)
-            row = dot(ones, jnp.concatenate([high, low], 1), ((1,), (1,)))
+            if which % 2:
+                row = jnp.sum(jnp.transpose(value), 0, keepdims=True)
+            else:
+                high = value.astype(jnp.bfloat16)
+                low = (value - high.astype(jnp.float32)).astype(jnp.bfloat16)
+                row = dot(ones, jnp.concatenate([high, low], 1), ((1,), (1,)))
             gathered[which, pl.ds(tile, 1), :] = row[0:1]
         return carry
 
-    lax.fori_loop(0, tiles, gather, 0, unroll=2)
+    lax.fori_loop(0, tiles, gather, 0, unroll=8)
     x, y, z = place[0], place[1], place[2]
     owner = iota((sectors * bins, LANES), 0) // bins
     lane = iota((1, LANES), 1)
@@ -295,7 +298,7 @@
         columns = pl.ds(pl.multiple_of(ib * PAIR_BLOCK, PAIR_BLOCK), PAIR_BLOCK)
         return pltpu.make_async_copy(out_ref.at[:, columns], out_hbm.at[:, columns], out_sem.at[ib])
 
-    lax.fori_loop(0, blocks, block_of, 0)
+    lax.fori_loop(0, blocks, block_of, 0, unroll=2)
     for ib in range(blocks):
         leave(ib).wait()
 

time: 45.3 us -> 43.3 us (0.956)
  Pallas kernels: 24.9 us -> 22 us
  waiting for transfers between devices: 5.51 us -> 6.34 us
    pallas_call x1, Pallas kernels: 12.9 us -> 11.3 us  [fast(): pl.pallas_call(functools.partial(wall_kernel, sectors, bins), out_shape=[...]
    all_to_all x1, waiting for transfers between devices: 5.5 us -> 6.18 us  [fast(): lax.all_to_all(outgoing, ('sector', 'bin'), split_axis=0, concat_axis=0,...]
    pallas_call x1, Pallas kernels: 1.84 us -> 1.17 us  [fast(): pl.pallas_call(functools.partial(facet_kernel, sectors), out_shape=pltpu....]
    pallas_call x1, Pallas kernels: 7.63 us -> 7.01 us  [fast(): pl.pallas_call(pair_kernel, out_shape=jax.ShapeDtypeStruct((7, slots), jn...]
  transfers between devices with their start and end apart: 5 -> 5, of which waited for: 1 -> 2; matrix products, arithmetic and copies ran while one was open for 0% -> 0% of each run, Pallas kernels for 27% -> 25%
where the time goes in v5:
time: 43.3 us; the launch traced here: 43 us
  Pallas kernels  22 us (51%)
  starting transfers between devices  13.4 us (31%)
  waiting for transfers between devices  6.34 us (15%)
  between operations  0.69 us (2%)
  other arithmetic  0.56 us (1%)
    pallas_call x1, Pallas kernels, fast(): pl.pallas_call(functools.partial(wall_kernel, sectors, bins), out_shape=[...  11.3 us
    pallas_call x1, Pallas kernels, fast(): pl.pallas_call(pair_kernel, out_shape=jax.ShapeDtypeStruct((7, slots), jn...  7.01 us
    all_to_all x1, starting transfers between devices, fast(): lax.all_to_all(outgoing, ('sector', 'bin'), split_axis=0, concat_axis=0,...  6.25 us
    all_to_all x1, waiting for transfers between devices, fast(): lax.all_to_all(outgoing, ('sector', 'bin'), split_axis=0, concat_axis=0,...  6.18 us
    ppermute x3, starting transfers between devices, fast(): lax.ppermute(block, 'sector', [(i, i ^ step) for i in range(sectors)])  4.63 us
    pallas_call x1, Pallas kernels, fast(): pl.pallas_call(pack_kernel, out_shape=pltpu.VMEM((words, LANES), jnp.floa...  2.54 us
    all_to_all x1, starting transfers between devices, fast(): lax.all_to_all(wrench.reshape(ndevices, 1, LANES), ('sector', 'bin'), spl...  2.48 us
    pallas_call x1, Pallas kernels, fast(): pl.pallas_call(functools.partial(facet_kernel, sectors), out_shape=pltpu....  1.17 us
  transfers between devices with their start and end apart: 5, of which 2 were waited for; matrix products, arithmetic and copies ran while one was open for 0% of the time, Pallas kernels for 25%

profile of v5, /device:TPU:0, one launch (start us, length us, event | category | flops | bytes accessed | tf_op | source)
XLA Modules:
  0.0 43.0 jit_solution(10671597338723807944)
XLA Ops:
  0.6 4.0 %collective-permute-start.2 = (f32[9,32,128]{2,1,0:T(8,128)}, f32[9,32,128]{2,1,0:T(8,128)S(1)}, u32[]{:S(2)}, u32[]{:S(2)}) collective-permute-start(f32[9,32,128]{2,1,0:T(8,128)} %bitcast.10), channel_id=1, source_target_pairs={{0,24},{8,16},{16,8},{24,0},{1,25},{9,17},{17,9},{25,1},{2,26},{10... | collective-permute-start | bytes 442376 | tf_op jit(solution)/shard_map/ppermute | solution.py:334
  4.6 0.5 %collective-permute-start.1 = (f32[9,32,128]{2,1,0:T(8,128)}, f32[9,32,128]{2,1,0:T(8,128)S(1)}, u32[]{:S(2)}, u32[]{:S(2)}) collective-permute-start(f32[9,32,128]{2,1,0:T(8,128)} %bitcast.11), channel_id=1, source_target_pairs={{0,16},{8,24},{16,0},{24,8},{1,17},{9,25},{17,1},{25,9},{2,18},{10... | collective-permute-start | bytes 442376 | tf_op jit(solution)/shard_map/ppermute | solution.py:334
  5.1 0.1 collective-permute-start
  5.3 2.5 %pack.1 = f32[128,128]{1,0:T(8,128)} custom-call(s32[8,128]{1,0:T(8,128)} %bitcast.14, f32[7,1024]{1,0:T(8,128)} %state_ref.1), custom_call_target="tpu_custom_call" | custom-call | tf_op jit(solution)/shard_map/pack/pallas_call | solution.py:326
  7.8 6.2 %all-to-all-start = ((f32[32,1,512]{2,1,0:T(1,128)}), f32[32,1,512]{2,1,0:T(1,128)S(1)}, u32[]{:S(2)}, u32[]{:S(2)}) async-start(f32[32,1,512]{2,1,0:T(1,128)} %bitcast.1), calls=%async_computation | async-start | bytes 131072 | tf_op jit(solution)/shard_map/all_to_all | solution.py:337
  14.1 0.0 collective-permute-done.2.refs_4_
  14.1 0.0 collective-permute-done.1.refs_3_
  14.1 0.0 collective-permute-done.refs_2_
  14.1 1.2 %facet.1.refs_2_ = f32[2,15,32,128]{3,2,1,0:T(8,128)S(1)} custom-call(s32[1,2]{1,0:T(1,128)} %refs_0_.3, f32[9,32,128]{2,1,0:T(8,128)} %bitcast.13, f32[9,32,128]{2,1,0:T(8,128)S(1)} %collective-permute-done.refs_2_, f32[9,32,128]{2,1,0:T(8,128)S(1)} %collective-permute-done.1.refs_3_, f32[9,32,128]{2,1,0:T(8,128)S(1)} %collective-permute-done.2.refs_4_), custom_call_target="tpu_custom_call" | custom-call | tf_op jit(solution)/shard_map/facet/pallas_call | solution.py:342
  15.3 6.2 %all-to-all-done = f32[32,1,512]{2,1,0:T(1,128)S(1)} async-done(((f32[32,1,512]{2,1,0:T(1,128)}), f32[32,1,512]{2,1,0:T(1,128)S(1)}, u32[]{:S(2)}, u32[]{:S(2)}) %all-to-all-start) | async-done | bytes 65568 | tf_op jit(solution)/shard_map/all_to_all | solution.py:337
  21.4 11.3 %wall.1 = (f32[32,128]{1,0:T(8,128)}, f32[3,16,128]{2,1,0:T(8,128)S(1)}, bf16[2048,128]{1,0:T(8,128)(2,1)S(1)}) custom-call(s32[1,2]{1,0:T(1,128)} %refs_0_.3, s32[1,2,32]{2,1,0:T(2,128)} %refs_1_.1, f32[2,15,32,128]{3,2,1,0:T(8,128)S(1)} %facet.1.refs_2_, f32[128,128]{1,0:T(8,128)S(1)} %bitcast.8), custom_call_target="tpu_custom_call" | custom-call | tf_op jit(solution)/shard_map/wall/pallas_call | solution.py:350
  32.8 2.5 %all-to-all-start.1 = ((f32[32,1,128]{2,1,0:T(1,128)}), f32[32,1,128]{2,1,0:T(1,128)S(1)}, u32[]{:S(2)}, u32[]{:S(2)}) async-start(f32[32,1,128]{2,1,0:T(1,128)} %bitcast.5), calls=%async_computation.1 | async-start | bytes 32768 | tf_op jit(solution)/shard_map/all_to_all | solution.py:367
  35.3 7.0 %pair.1 = f32[7,2048]{1,0:T(8,128)} custom-call(f32[128,128]{1,0:T(8,128)S(1)} %bitcast.9, f32[3,16,128]{2,1,0:T(8,128)S(1)} %get-tuple-element.5.force_ref, bf16[2048,128]{1,0:T(8,128)(2,1)S(1)} %get-tuple-element.6.left), custom_call_target="tpu_custom_call" | custom-call | tf_op jit(solution)/shard_map/pair/pallas_call | solution.py:370
  42.3 0.2 all-to-all-done.1
  42.4 0.6 %slice_reduce_fusion = f32[6]{0:T(128)} fusion(f32[32,1,128]{2,1,0:T(1,128)S(1)} %all-to-all-done.1), kind=kLoop, calls=%fused_computation | loop fusion | flops 186 | bytes 792 | tf_op jit(solution)/shard_map/reduce_sum | solution.py:383
Async XLA Ops:
  0.6 13.4 %collective-permute-start.2 = (f32[9,32,128]{2,1,0:T(8,128)}, f32[9,32,128]{2,1,0:T(8,128)S(1)}, u32[]{:S(2)}, u32[]{:S(2)}) collective-permute-start(f32[9,32,128]{2,1,0:T(8,128)} %bitcast.10), channel_id=1, source_target_pairs={{0,24},{8,16},{16,8},{24,0},{1,25},{9,17},{17,9},{25,1},{2,26},{10... | collective-permute-start | bytes 442376 | tf_op jit(solution)/shard_map/ppermute | solution.py:334
  4.6 9.5 %collective-permute-start.1 = (f32[9,32,128]{2,1,0:T(8,128)}, f32[9,32,128]{2,1,0:T(8,128)S(1)}, u32[]{:S(2)}, u32[]{:S(2)}) collective-permute-start(f32[9,32,128]{2,1,0:T(8,128)} %bitcast.11), channel_id=1, source_target_pairs={{0,16},{8,24},{16,0},{24,8},{1,17},{9,25},{17,1},{25,9},{2,18},{10... | collective-permute-start | bytes 442376 | tf_op jit(solution)/shard_map/ppermute | solution.py:334
  5.1 9.0 %collective-permute-start = (f32[9,32,128]{2,1,0:T(8,128)}, f32[9,32,128]{2,1,0:T(8,128)S(1)}, u32[]{:S(2)}, u32[]{:S(2)}) collective-permute-start(f32[9,32,128]{2,1,0:T(8,128)} %bitcast.12), channel_id=1, source_target_pairs={{0,8},{8,0},{16,24},{24,16},{1,9},{9,1},{17,25},{25,17},{2,10},{10... | collective-permute-start | bytes 442376 | tf_op jit(solution)/shard_map/ppermute | solution.py:334
  7.8 13.6 %all-to-all-start = ((f32[32,1,512]{2,1,0:T(1,128)}), f32[32,1,512]{2,1,0:T(1,128)S(1)}, u32[]{:S(2)}, u32[]{:S(2)}) async-start(f32[32,1,512]{2,1,0:T(1,128)} %bitcast.1), calls=%async_computation | async-start | bytes 131072 | tf_op jit(solution)/shard_map/all_to_all | solution.py:337
  32.8 9.7 %all-to-all-start.1 = ((f32[32,1,128]{2,1,0:T(1,128)}), f32[32,1,128]{2,1,0:T(1,128)S(1)}, u32[]{:S(2)}, u32[]{:S(2)}) async-start(f32[32,1,128]{2,1,0:T(1,128)} %bitcast.5), calls=%async_computation.1 | async-start | bytes 32768 | tf_op jit(solution)/shard_map/all_to_all | solution.py:367

commit v6 on v5

--- a/solution.py
+++ b/solution.py
@@ -17,7 +17,7 @@
 
 LANES = 128
 PAYLOAD = ((0, 3), (1, 4), (2, 5), (6, None))
-PAIR_BLOCK = 512
+PAIR_BLOCK = 1024
 SPREAD = 4
 
 
@@ -41,21 +41,18 @@
     ndevices = out_ref.shape[0] * LANES // (8 * 64)
     capacity = 64
     dest = dest_ref[...]
-    wide = blocks * ndevices
-    expand = (iota((blocks, wide), 1) // ndevices == iota((blocks, wide), 0)).astype(jnp.bfloat16)
-    dest_cols = jnp.transpose(dest.astype(jnp.float32)).astype(jnp.bfloat16)
-    named = dot(dest_cols, expand)
-    onehot = (named == (iota((LANES, wide), 1) % ndevices).astype(jnp.float32)).astype(jnp.float32)
-    lower = (iota((LANES, LANES), 0) >= iota((LANES, LANES), 1)).astype(jnp.bfloat16)
-    counted = dot(lower, onehot.astype(jnp.bfloat16))
-    total = jnp.broadcast_to(counted[LANES - 1 :], (8, wide))
-    before = jnp.zeros((8, wide), jnp.float32)
-    for step in range(1, blocks):
-        moved = pltpu.roll(total, step * ndevices, 1)
-        before = before + jnp.where(iota((8, wide), 1) >= step * ndevices, moved, 0.0)
-    place = (onehot * (counted - 1.0 + before[0:1])).astype(jnp.bfloat16)
-    ranks = dot(expand, place, ((1,), (1,)))
-    rank_row = jnp.concatenate([ranks[b : b + 1] for b in range(blocks)], 1)
+    upper = (iota((LANES, LANES), 0) <= iota((LANES, LANES), 1)).astype(jnp.bfloat16)
+    named = [
+        (dest[b : b + 1] == iota((ndevices, LANES), 0)).astype(jnp.float32) for b in range(blocks)
+    ]
+    counted = dot(jnp.concatenate(named, 0).astype(jnp.bfloat16), upper)
+    before = jnp.full((ndevices, LANES), -1.0, jnp.float32)
+    ranks = []
+    for b in range(blocks):
+        mine = counted[b * ndevices : (b + 1) * ndevices]
+        ranks.append(jnp.sum(named[b] * (mine + before), 0, keepdims=True))
+        before = before + jnp.broadcast_to(mine[:, LANES - 1 :], (ndevices, LANES))
+    rank_row = jnp.concatenate(ranks, 1)
     dest_row = jnp.concatenate([dest[b : b + 1] for b in range(blocks)], 1)
     leaving = blocks * LANES
     chosen = dest_row == iota((ndevices, leaving), 0)
@@ -298,7 +295,7 @@
         columns = pl.ds(pl.multiple_of(ib * PAIR_BLOCK, PAIR_BLOCK), PAIR_BLOCK)
         return pltpu.make_async_copy(out_ref.at[:, columns], out_hbm.at[:, columns], out_sem.at[ib])
 
-    lax.fori_loop(0, blocks, block_of, 0, unroll=2)
+    lax.fori_loop(0, blocks, block_of, 0)
     for ib in range(blocks):
         leave(ib).wait()
 

time: 43.3 us -> 42.9 us (level)
  Pallas kernels: 22 us -> 21 us
  waiting for transfers between devices: 6.34 us -> 7.06 us
    pallas_call x1, Pallas kernels: 7.01 us -> 6.29 us  [fast(): pl.pallas_call(pair_kernel, out_shape=jax.ShapeDtypeStruct((7, slots), jn...]
    all_to_all x1, waiting for transfers between devices: 0.16 us -> 0.88 us  [fast(): lax.all_to_all(wrench.reshape(ndevices, 1, LANES), ('sector', 'bin'), spl...]
  transfers between devices with their start and end apart: 5 -> 5, of which waited for: 2 -> 2; matrix products, arithmetic and copies ran while one was open for 0% -> 0% of each run, Pallas kernels for 25% -> 23%
where the time goes in v6:
time: 42.9 us; the launch traced here: 42.6 us
  Pallas kernels  21 us (49%)
  starting transfers between devices  13.4 us (31%)
  waiting for transfers between devices  7.06 us (16%)
  between operations  0.69 us (2%)
  other arithmetic  0.56 us (1%)
    pallas_call x1, Pallas kernels, fast(): pl.pallas_call(functools.partial(wall_kernel, sectors, bins), out_shape=[...  11.4 us
    pallas_call x1, Pallas kernels, fast(): pl.pallas_call(pair_kernel, out_shape=jax.ShapeDtypeStruct((7, slots), jn...  6.29 us
    all_to_all x1, starting transfers between devices, fast(): lax.all_to_all(outgoing, ('sector', 'bin'), split_axis=0, concat_axis=0,...  6.24 us
    all_to_all x1, waiting for transfers between devices, fast(): lax.all_to_all(outgoing, ('sector', 'bin'), split_axis=0, concat_axis=0,...  6.18 us
    ppermute x3, starting transfers between devices, fast(): lax.ppermute(block, 'sector', [(i, i ^ step) for i in range(sectors)])  4.63 us
    all_to_all x1, starting transfers between devices, fast(): lax.all_to_all(wrench.reshape(ndevices, 1, LANES), ('sector', 'bin'), spl...  2.48 us
    pallas_call x1, Pallas kernels, fast(): pl.pallas_call(pack_kernel, out_shape=pltpu.VMEM((words, LANES), jnp.floa...  2.17 us
    pallas_call x1, Pallas kernels, fast(): pl.pallas_call(functools.partial(facet_kernel, sectors), out_shape=pltpu....  1.17 us
  transfers between devices with their start and end apart: 5, of which 2 were waited for; matrix products, arithmetic and copies ran while one was open for 0% of the time, Pallas kernels for 23%

profile of v6, /device:TPU:0, one launch (start us, length us, event | category | flops | bytes accessed | tf_op | source)
XLA Modules:
  0.0 42.6 jit_solution(6388263423048196472)
XLA Ops:
  0.6 4.0 %collective-permute-start.2 = (f32[9,32,128]{2,1,0:T(8,128)}, f32[9,32,128]{2,1,0:T(8,128)S(1)}, u32[]{:S(2)}, u32[]{:S(2)}) collective-permute-start(f32[9,32,128]{2,1,0:T(8,128)} %bitcast.10), channel_id=1, source_target_pairs={{0,24},{8,16},{16,8},{24,0},{1,25},{9,17},{17,9},{25,1},{2,26},{10... | collective-permute-start | bytes 442376 | tf_op jit(solution)/shard_map/ppermute | solution.py:331
  4.6 0.5 %collective-permute-start.1 = (f32[9,32,128]{2,1,0:T(8,128)}, f32[9,32,128]{2,1,0:T(8,128)S(1)}, u32[]{:S(2)}, u32[]{:S(2)}) collective-permute-start(f32[9,32,128]{2,1,0:T(8,128)} %bitcast.11), channel_id=1, source_target_pairs={{0,16},{8,24},{16,0},{24,8},{1,17},{9,25},{17,1},{25,9},{2,18},{10... | collective-permute-start | bytes 442376 | tf_op jit(solution)/shard_map/ppermute | solution.py:331
  5.1 0.1 collective-permute-start
  5.3 2.2 %pack.1 = f32[128,128]{1,0:T(8,128)} custom-call(s32[8,128]{1,0:T(8,128)} %bitcast.14, f32[7,1024]{1,0:T(8,128)} %state_ref.1), custom_call_target="tpu_custom_call" | custom-call | tf_op jit(solution)/shard_map/pack/pallas_call | solution.py:323
  7.4 6.2 %all-to-all-start = ((f32[32,1,512]{2,1,0:T(1,128)}), f32[32,1,512]{2,1,0:T(1,128)S(1)}, u32[]{:S(2)}, u32[]{:S(2)}) async-start(f32[32,1,512]{2,1,0:T(1,128)} %bitcast.1), calls=%async_computation | async-start | bytes 131072 | tf_op jit(solution)/shard_map/all_to_all | solution.py:334
  13.7 0.0 collective-permute-done.2.refs_4_
  13.7 0.0 collective-permute-done.1.refs_3_
  13.7 0.0 collective-permute-done.refs_2_
  13.7 1.2 %facet.1.refs_2_ = f32[2,15,32,128]{3,2,1,0:T(8,128)S(1)} custom-call(s32[1,2]{1,0:T(1,128)} %refs_0_.3, f32[9,32,128]{2,1,0:T(8,128)} %bitcast.13, f32[9,32,128]{2,1,0:T(8,128)S(1)} %collective-permute-done.refs_2_, f32[9,32,128]{2,1,0:T(8,128)S(1)} %collective-permute-done.1.refs_3_, f32[9,32,128]{2,1,0:T(8,128)S(1)} %collective-permute-done.2.refs_4_), custom_call_target="tpu_custom_call" | custom-call | tf_op jit(solution)/shard_map/facet/pallas_call | solution.py:339
  14.9 6.2 %all-to-all-done = f32[32,1,512]{2,1,0:T(1,128)S(1)} async-done(((f32[32,1,512]{2,1,0:T(1,128)}), f32[32,1,512]{2,1,0:T(1,128)S(1)}, u32[]{:S(2)}, u32[]{:S(2)}) %all-to-all-start) | async-done | bytes 65568 | tf_op jit(solution)/shard_map/all_to_all | solution.py:334
  21.1 11.4 %wall.1 = (f32[32,128]{1,0:T(8,128)}, f32[3,16,128]{2,1,0:T(8,128)S(1)}, bf16[2048,128]{1,0:T(8,128)(2,1)S(1)}) custom-call(s32[1,2]{1,0:T(1,128)} %refs_0_.3, s32[1,2,32]{2,1,0:T(2,128)} %refs_1_.1, f32[2,15,32,128]{3,2,1,0:T(8,128)S(1)} %facet.1.refs_2_, f32[128,128]{1,0:T(8,128)S(1)} %bitcast.8), custom_call_target="tpu_custom_call" | custom-call | tf_op jit(solution)/shard_map/wall/pallas_call | solution.py:347
  32.4 2.5 %all-to-all-start.1 = ((f32[32,1,128]{2,1,0:T(1,128)}), f32[32,1,128]{2,1,0:T(1,128)S(1)}, u32[]{:S(2)}, u32[]{:S(2)}) async-start(f32[32,1,128]{2,1,0:T(1,128)} %bitcast.5), calls=%async_computation.1 | async-start | bytes 32768 | tf_op jit(solution)/shard_map/all_to_all | solution.py:364
  34.9 6.3 %pair.1 = f32[7,2048]{1,0:T(8,128)} custom-call(f32[128,128]{1,0:T(8,128)S(1)} %bitcast.9, f32[3,16,128]{2,1,0:T(8,128)S(1)} %get-tuple-element.5.force_ref, bf16[2048,128]{1,0:T(8,128)(2,1)S(1)} %get-tuple-element.6.left), custom_call_target="tpu_custom_call" | custom-call | tf_op jit(solution)/shard_map/pair/pallas_call | solution.py:367
  41.2 0.9 %all-to-all-done.1 = f32[32,1,128]{2,1,0:T(1,128)S(1)} async-done(((f32[32,1,128]{2,1,0:T(1,128)}), f32[32,1,128]{2,1,0:T(1,128)S(1)}, u32[]{:S(2)}, u32[]{:S(2)}) %all-to-all-start.1) | async-done | bytes 16416 | tf_op jit(solution)/shard_map/all_to_all | solution.py:364
  42.1 0.6 %slice_reduce_fusion = f32[6]{0:T(128)} fusion(f32[32,1,128]{2,1,0:T(1,128)S(1)} %all-to-all-done.1), kind=kLoop, calls=%fused_computation | loop fusion | flops 186 | bytes 792 | tf_op jit(solution)/shard_map/reduce_sum | solution.py:380
Async XLA Ops:
  0.6 13.1 %collective-permute-start.2 = (f32[9,32,128]{2,1,0:T(8,128)}, f32[9,32,128]{2,1,0:T(8,128)S(1)}, u32[]{:S(2)}, u32[]{:S(2)}) collective-permute-start(f32[9,32,128]{2,1,0:T(8,128)} %bitcast.10), channel_id=1, source_target_pairs={{0,24},{8,16},{16,8},{24,0},{1,25},{9,17},{17,9},{25,1},{2,26},{10... | collective-permute-start | bytes 442376 | tf_op jit(solution)/shard_map/ppermute | solution.py:331
  4.6 9.1 %collective-permute-start.1 = (f32[9,32,128]{2,1,0:T(8,128)}, f32[9,32,128]{2,1,0:T(8,128)S(1)}, u32[]{:S(2)}, u32[]{:S(2)}) collective-permute-start(f32[9,32,128]{2,1,0:T(8,128)} %bitcast.11), channel_id=1, source_target_pairs={{0,16},{8,24},{16,0},{24,8},{1,17},{9,25},{17,1},{25,9},{2,18},{10... | collective-permute-start | bytes 442376 | tf_op jit(solution)/shard_map/ppermute | solution.py:331
  5.1 8.6 %collective-permute-start = (f32[9,32,128]{2,1,0:T(8,128)}, f32[9,32,128]{2,1,0:T(8,128)S(1)}, u32[]{:S(2)}, u32[]{:S(2)}) collective-permute-start(f32[9,32,128]{2,1,0:T(8,128)} %bitcast.12), channel_id=1, source_target_pairs={{0,8},{8,0},{16,24},{24,16},{1,9},{9,1},{17,25},{25,17},{2,10},{10... | collective-permute-start | bytes 442376 | tf_op jit(solution)/shard_map/ppermute | solution.py:331
  7.4 13.6 %all-to-all-start = ((f32[32,1,512]{2,1,0:T(1,128)}), f32[32,1,512]{2,1,0:T(1,128)S(1)}, u32[]{:S(2)}, u32[]{:S(2)}) async-start(f32[32,1,512]{2,1,0:T(1,128)} %bitcast.1), calls=%async_computation | async-start | bytes 131072 | tf_op jit(solution)/shard_map/all_to_all | solution.py:334
  32.4 9.7 %all-to-all-start.1 = ((f32[32,1,128]{2,1,0:T(1,128)}), f32[32,1,128]{2,1,0:T(1,128)S(1)}, u32[]{:S(2)}, u32[]{:S(2)}) async-start(f32[32,1,128]{2,1,0:T(1,128)} %bitcast.5), calls=%async_computation.1 | async-start | bytes 32768 | tf_op jit(solution)/shard_map/all_to_all | solution.py:364

commit v7 on v6

--- a/solution.py
+++ b/solution.py
@@ -19,6 +19,7 @@
 PAYLOAD = ((0, 3), (1, 4), (2, 5), (6, None))
 PAIR_BLOCK = 1024
 SPREAD = 4
+WALL_ROWS = 64
 
 
 def iota(shape, dim):
@@ -179,23 +180,24 @@
         first = pl.multiple_of(quotient(code, tiles_tri) * LANES, LANES)
         facet_tile = remainder(code, tiles_tri)
         f = [facet[entry, i, pl.ds(facet_tile, 1), :] for i in range(15)]
-        at = pl.ds(first, LANES)
-        dx, dy, dz = spread[0, at, :] - f[0], spread[1, at, :] - f[1], spread[2, at, :] - f[2]
-        beta = dx * f[9] + dy * f[10] + dz * f[11]
-        gamma = dx * f[12] + dy * f[13] + dz * f[14]
-        alpha = jnp.maximum(1.0 - beta - gamma, 0.0)
-        beta = jnp.maximum(beta, 0.0)
-        gamma = jnp.maximum(gamma, 0.0)
-        scale = 1.0 / (alpha + beta + gamma)
-        beta = beta * scale
-        gamma = gamma * scale
-        ox = dx - beta * f[3] - gamma * f[6]
-        oy = dy - beta * f[4] - gamma * f[7]
-        oz = dz - beta * f[5] - gamma * f[8]
-        deep = jnp.maximum(spread[3, at, :] - (ox * ox + oy * oy + oz * oz), 0.0)
-        accs[3 * entry][at, :] += deep * ox
-        accs[3 * entry + 1][at, :] += deep * oy
-        accs[3 * entry + 2][at, :] += deep * oz
+        for part in range(LANES // WALL_ROWS):
+            at = pl.ds(pl.multiple_of(first + part * WALL_ROWS, WALL_ROWS), WALL_ROWS)
+            dx, dy, dz = spread[0, at, :] - f[0], spread[1, at, :] - f[1], spread[2, at, :] - f[2]
+            beta = dx * f[9] + dy * f[10] + dz * f[11]
+            gamma = dx * f[12] + dy * f[13] + dz * f[14]
+            alpha = jnp.maximum(1.0 - beta - gamma, 0.0)
+            beta = jnp.maximum(beta, 0.0)
+            gamma = jnp.maximum(gamma, 0.0)
+            scale = 1.0 / (alpha + beta + gamma)
+            beta = beta * scale
+            gamma = gamma * scale
+            ox = dx - beta * f[3] - gamma * f[6]
+            oy = dy - beta * f[4] - gamma * f[7]
+            oz = dz - beta * f[5] - gamma * f[8]
+            deep = jnp.maximum(spread[3, at, :] - (ox * ox + oy * oy + oz * oz), 0.0)
+            accs[3 * entry][at, :] += deep * ox
+            accs[3 * entry + 1][at, :] += deep * oy
+            accs[3 * entry + 2][at, :] += deep * oz
 
     def step(number, carry):
         for entry in range(entries):

time: 42.9 us -> 42.7 us (level)
  waiting for transfers between devices: 7.06 us -> 6.38 us
    all_to_all x1, waiting for transfers between devices: 6.18 us -> 5.5 us  [fast(): lax.all_to_all(outgoing, ('sector', 'bin'), split_axis=0, concat_axis=0,...]
    pallas_call x1, Pallas kernels: 1.17 us -> 1.84 us  [fast(): pl.pallas_call(functools.partial(facet_kernel, sectors), out_shape=pltpu....]
  transfers between devices with their start and end apart: 5 -> 5, of which waited for: 2 -> 2; matrix products, arithmetic and copies ran while one was open for 0% -> 0% of each run, Pallas kernels for 23% -> 24%
where the time goes in v7:
time: 42.7 us; the launch traced here: 42.4 us
  Pallas kernels  21.4 us (50%)
  starting transfers between devices  13.4 us (31%)
  waiting for transfers between devices  6.38 us (15%)
  between operations  0.69 us (2%)
  other arithmetic  0.56 us (1%)
    pallas_call x1, Pallas kernels, fast(): pl.pallas_call(functools.partial(wall_kernel, sectors, bins), out_shape=[...  11.1 us
    pallas_call x1, Pallas kernels, fast(): pl.pallas_call(pair_kernel, out_shape=jax.ShapeDtypeStruct((7, slots), jn...  6.3 us
    all_to_all x1, starting transfers between devices, fast(): lax.all_to_all(outgoing, ('sector', 'bin'), split_axis=0, concat_axis=0,...  6.24 us
    all_to_all x1, waiting for transfers between devices, fast(): lax.all_to_all(outgoing, ('sector', 'bin'), split_axis=0, concat_axis=0,...  5.5 us
    ppermute x3, starting transfers between devices, fast(): lax.ppermute(block, 'sector', [(i, i ^ step) for i in range(sectors)])  4.63 us
    all_to_all x1, starting transfers between devices, fast(): lax.all_to_all(wrench.reshape(ndevices, 1, LANES), ('sector', 'bin'), spl...  2.48 us
    pallas_call x1, Pallas kernels, fast(): pl.pallas_call(pack_kernel, out_shape=pltpu.VMEM((words, LANES), jnp.floa...  2.17 us
    pallas_call x1, Pallas kernels, fast(): pl.pallas_call(functools.partial(facet_kernel, sectors), out_shape=pltpu....  1.84 us
  transfers between devices with their start and end apart: 5, of which 2 were waited for; matrix products, arithmetic and copies ran while one was open for 0% of the time, Pallas kernels for 24%

profile of v7, /device:TPU:0, one launch (start us, length us, event | category | flops | bytes accessed | tf_op | source)
XLA Modules:
  0.0 42.4 jit_solution(12583512268380410500)
XLA Ops:
  0.6 4.0 %collective-permute-start.2 = (f32[9,32,128]{2,1,0:T(8,128)}, f32[9,32,128]{2,1,0:T(8,128)S(1)}, u32[]{:S(2)}, u32[]{:S(2)}) collective-permute-start(f32[9,32,128]{2,1,0:T(8,128)} %bitcast.10), channel_id=1, source_target_pairs={{0,24},{8,16},{16,8},{24,0},{1,25},{9,17},{17,9},{25,1},{2,26},{10... | collective-permute-start | bytes 442376 | tf_op jit(solution)/shard_map/ppermute | solution.py:333
  4.6 0.5 %collective-permute-start.1 = (f32[9,32,128]{2,1,0:T(8,128)}, f32[9,32,128]{2,1,0:T(8,128)S(1)}, u32[]{:S(2)}, u32[]{:S(2)}) collective-permute-start(f32[9,32,128]{2,1,0:T(8,128)} %bitcast.11), channel_id=1, source_target_pairs={{0,16},{8,24},{16,0},{24,8},{1,17},{9,25},{17,1},{25,9},{2,18},{10... | collective-permute-start | bytes 442376 | tf_op jit(solution)/shard_map/ppermute | solution.py:333
  5.1 0.1 collective-permute-start
  5.3 2.2 %pack.1 = f32[128,128]{1,0:T(8,128)} custom-call(s32[8,128]{1,0:T(8,128)} %bitcast.14, f32[7,1024]{1,0:T(8,128)} %state_ref.1), custom_call_target="tpu_custom_call" | custom-call | tf_op jit(solution)/shard_map/pack/pallas_call | solution.py:325
  7.4 6.2 %all-to-all-start = ((f32[32,1,512]{2,1,0:T(1,128)}), f32[32,1,512]{2,1,0:T(1,128)S(1)}, u32[]{:S(2)}, u32[]{:S(2)}) async-start(f32[32,1,512]{2,1,0:T(1,128)} %bitcast.1), calls=%async_computation | async-start | bytes 131072 | tf_op jit(solution)/shard_map/all_to_all | solution.py:336
  13.7 0.0 collective-permute-done.2.refs_4_
  13.7 0.0 collective-permute-done.1.refs_3_
  13.7 0.0 collective-permute-done.refs_2_
  13.7 1.8 %facet.1.refs_2_ = f32[2,15,32,128]{3,2,1,0:T(8,128)S(1)} custom-call(s32[1,2]{1,0:T(1,128)} %refs_0_.3, f32[9,32,128]{2,1,0:T(8,128)} %bitcast.13, f32[9,32,128]{2,1,0:T(8,128)S(1)} %collective-permute-done.refs_2_, f32[9,32,128]{2,1,0:T(8,128)S(1)} %collective-permute-done.1.refs_3_, f32[9,32,128]{2,1,0:T(8,128)S(1)} %collective-permute-done.2.refs_4_), custom_call_target="tpu_custom_call" | custom-call | tf_op jit(solution)/shard_map/facet/pallas_call | solution.py:341
  15.6 5.5 %all-to-all-done = f32[32,1,512]{2,1,0:T(1,128)S(1)} async-done(((f32[32,1,512]{2,1,0:T(1,128)}), f32[32,1,512]{2,1,0:T(1,128)S(1)}, u32[]{:S(2)}, u32[]{:S(2)}) %all-to-all-start) | async-done | bytes 65568 | tf_op jit(solution)/shard_map/all_to_all | solution.py:336
  21.1 11.1 %wall.1 = (f32[32,128]{1,0:T(8,128)}, f32[3,16,128]{2,1,0:T(8,128)S(1)}, bf16[2048,128]{1,0:T(8,128)(2,1)S(1)}) custom-call(s32[1,2]{1,0:T(1,128)} %refs_0_.3, s32[1,2,32]{2,1,0:T(2,128)} %refs_1_.1, f32[2,15,32,128]{3,2,1,0:T(8,128)S(1)} %facet.1.refs_2_, f32[128,128]{1,0:T(8,128)S(1)} %bitcast.8), custom_call_target="tpu_custom_call" | custom-call | tf_op jit(solution)/shard_map/wall/pallas_call | solution.py:349
  32.2 2.5 %all-to-all-start.1 = ((f32[32,1,128]{2,1,0:T(1,128)}), f32[32,1,128]{2,1,0:T(1,128)S(1)}, u32[]{:S(2)}, u32[]{:S(2)}) async-start(f32[32,1,128]{2,1,0:T(1,128)} %bitcast.5), calls=%async_computation.1 | async-start | bytes 32768 | tf_op jit(solution)/shard_map/all_to_all | solution.py:366
  34.7 6.3 %pair.1 = f32[7,2048]{1,0:T(8,128)} custom-call(f32[128,128]{1,0:T(8,128)S(1)} %bitcast.9, f32[3,16,128]{2,1,0:T(8,128)S(1)} %get-tuple-element.5.force_ref, bf16[2048,128]{1,0:T(8,128)(2,1)S(1)} %get-tuple-element.6.left), custom_call_target="tpu_custom_call" | custom-call | tf_op jit(solution)/shard_map/pair/pallas_call | solution.py:369
  41.0 0.9 %all-to-all-done.1 = f32[32,1,128]{2,1,0:T(1,128)S(1)} async-done(((f32[32,1,128]{2,1,0:T(1,128)}), f32[32,1,128]{2,1,0:T(1,128)S(1)}, u32[]{:S(2)}, u32[]{:S(2)}) %all-to-all-start.1) | async-done | bytes 16416 | tf_op jit(solution)/shard_map/all_to_all | solution.py:366
  41.9 0.6 %slice_reduce_fusion = f32[6]{0:T(128)} fusion(f32[32,1,128]{2,1,0:T(1,128)S(1)} %all-to-all-done.1), kind=kLoop, calls=%fused_computation | loop fusion | flops 186 | bytes 792 | tf_op jit(solution)/shard_map/reduce_sum | solution.py:382
Async XLA Ops:
  0.6 13.1 %collective-permute-start.2 = (f32[9,32,128]{2,1,0:T(8,128)}, f32[9,32,128]{2,1,0:T(8,128)S(1)}, u32[]{:S(2)}, u32[]{:S(2)}) collective-permute-start(f32[9,32,128]{2,1,0:T(8,128)} %bitcast.10), channel_id=1, source_target_pairs={{0,24},{8,16},{16,8},{24,0},{1,25},{9,17},{17,9},{25,1},{2,26},{10... | collective-permute-start | bytes 442376 | tf_op jit(solution)/shard_map/ppermute | solution.py:333
  4.6 9.1 %collective-permute-start.1 = (f32[9,32,128]{2,1,0:T(8,128)}, f32[9,32,128]{2,1,0:T(8,128)S(1)}, u32[]{:S(2)}, u32[]{:S(2)}) collective-permute-start(f32[9,32,128]{2,1,0:T(8,128)} %bitcast.11), channel_id=1, source_target_pairs={{0,16},{8,24},{16,0},{24,8},{1,17},{9,25},{17,1},{25,9},{2,18},{10... | collective-permute-start | bytes 442376 | tf_op jit(solution)/shard_map/ppermute | solution.py:333
  5.1 8.6 %collective-permute-start = (f32[9,32,128]{2,1,0:T(8,128)}, f32[9,32,128]{2,1,0:T(8,128)S(1)}, u32[]{:S(2)}, u32[]{:S(2)}) collective-permute-start(f32[9,32,128]{2,1,0:T(8,128)} %bitcast.12), channel_id=1, source_target_pairs={{0,8},{8,0},{16,24},{24,16},{1,9},{9,1},{17,25},{25,17},{2,10},{10... | collective-permute-start | bytes 442376 | tf_op jit(solution)/shard_map/ppermute | solution.py:333
  7.4 13.6 %all-to-all-start = ((f32[32,1,512]{2,1,0:T(1,128)}), f32[32,1,512]{2,1,0:T(1,128)S(1)}, u32[]{:S(2)}, u32[]{:S(2)}) async-start(f32[32,1,512]{2,1,0:T(1,128)} %bitcast.1), calls=%async_computation | async-start | bytes 131072 | tf_op jit(solution)/shard_map/all_to_all | solution.py:336
  32.2 9.7 %all-to-all-start.1 = ((f32[32,1,128]{2,1,0:T(1,128)}), f32[32,1,128]{2,1,0:T(1,128)S(1)}, u32[]{:S(2)}, u32[]{:S(2)}) async-start(f32[32,1,128]{2,1,0:T(1,128)} %bitcast.5), calls=%async_computation.1 | async-start | bytes 32768 | tf_op jit(solution)/shard_map/all_to_all | solution.py:366

commit v8 on v7

--- a/solution.py
+++ b/solution.py
@@ -18,7 +18,7 @@
 LANES = 128
 PAYLOAD = ((0, 3), (1, 4), (2, 5), (6, None))
 PAIR_BLOCK = 1024
-SPREAD = 4
+SPREAD = 2
 WALL_ROWS = 64
 
 
@@ -221,7 +221,7 @@
             gathered[which, pl.ds(tile, 1), :] = row[0:1]
         return carry
 
-    lax.fori_loop(0, tiles, gather, 0, unroll=8)
+    lax.fori_loop(0, tiles, gather, 0, unroll=16)
     x, y, z = place[0], place[1], place[2]
     owner = iota((sectors * bins, LANES), 0) // bins
     lane = iota((1, LANES), 1)

time: 42.7 us -> 42.6 us (level)
  no operation moved by 1% of the time
where the time goes in v8:
time: 42.6 us; the launch traced here: 42.3 us
  Pallas kernels  21.3 us (50%)
  starting transfers between devices  13.4 us (31%)
  waiting for transfers between devices  6.39 us (15%)
  between operations  0.69 us (2%)
  other arithmetic  0.56 us (1%)
    pallas_call x1, Pallas kernels, fast(): pl.pallas_call(functools.partial(wall_kernel, sectors, bins), out_shape=[...  11 us
    pallas_call x1, Pallas kernels, fast(): pl.pallas_call(pair_kernel, out_shape=jax.ShapeDtypeStruct((7, slots), jn...  6.29 us
    all_to_all x1, starting transfers between devices, fast(): lax.all_to_all(outgoing, ('sector', 'bin'), split_axis=0, concat_axis=0,...  6.24 us
    all_to_all x1, waiting for transfers between devices, fast(): lax.all_to_all(outgoing, ('sector', 'bin'), split_axis=0, concat_axis=0,...  5.5 us
    ppermute x3, starting transfers between devices, fast(): lax.ppermute(block, 'sector', [(i, i ^ step) for i in range(sectors)])  4.63 us
    all_to_all x1, starting transfers between devices, fast(): lax.all_to_all(wrench.reshape(ndevices, 1, LANES), ('sector', 'bin'), spl...  2.48 us
    pallas_call x1, Pallas kernels, fast(): pl.pallas_call(pack_kernel, out_shape=pltpu.VMEM((words, LANES), jnp.floa...  2.17 us
    pallas_call x1, Pallas kernels, fast(): pl.pallas_call(functools.partial(facet_kernel, sectors), out_shape=pltpu....  1.84 us
  transfers between devices with their start and end apart: 5, of which 2 were waited for; matrix products, arithmetic and copies ran while one was open for 0% of the time, Pallas kernels for 24%

profile of v8, /device:TPU:0, one launch (start us, length us, event | category | flops | bytes accessed | tf_op | source)
XLA Modules:
  0.0 42.3 jit_solution(5713003333790481179)
XLA Ops:
  0.6 4.0 %collective-permute-start.2 = (f32[9,32,128]{2,1,0:T(8,128)}, f32[9,32,128]{2,1,0:T(8,128)S(1)}, u32[]{:S(2)}, u32[]{:S(2)}) collective-permute-start(f32[9,32,128]{2,1,0:T(8,128)} %bitcast.10), channel_id=1, source_target_pairs={{0,24},{8,16},{16,8},{24,0},{1,25},{9,17},{17,9},{25,1},{2,26},{10... | collective-permute-start | bytes 442376 | tf_op jit(solution)/shard_map/ppermute | solution.py:333
  4.6 0.5 %collective-permute-start.1 = (f32[9,32,128]{2,1,0:T(8,128)}, f32[9,32,128]{2,1,0:T(8,128)S(1)}, u32[]{:S(2)}, u32[]{:S(2)}) collective-permute-start(f32[9,32,128]{2,1,0:T(8,128)} %bitcast.11), channel_id=1, source_target_pairs={{0,16},{8,24},{16,0},{24,8},{1,17},{9,25},{17,1},{25,9},{2,18},{10... | collective-permute-start | bytes 442376 | tf_op jit(solution)/shard_map/ppermute | solution.py:333
  5.1 0.1 collective-permute-start
  5.3 2.2 %pack.1 = f32[128,128]{1,0:T(8,128)} custom-call(s32[8,128]{1,0:T(8,128)} %bitcast.14, f32[7,1024]{1,0:T(8,128)} %state_ref.1), custom_call_target="tpu_custom_call" | custom-call | tf_op jit(solution)/shard_map/pack/pallas_call | solution.py:325
  7.4 6.2 %all-to-all-start = ((f32[32,1,512]{2,1,0:T(1,128)}), f32[32,1,512]{2,1,0:T(1,128)S(1)}, u32[]{:S(2)}, u32[]{:S(2)}) async-start(f32[32,1,512]{2,1,0:T(1,128)} %bitcast.1), calls=%async_computation | async-start | bytes 131072 | tf_op jit(solution)/shard_map/all_to_all | solution.py:336
  13.7 0.0 collective-permute-done.2.refs_4_
  13.7 0.0 collective-permute-done.1.refs_3_
  13.7 0.0 collective-permute-done.refs_2_
  13.7 1.8 %facet.1.refs_2_ = f32[2,15,32,128]{3,2,1,0:T(8,128)S(1)} custom-call(s32[1,2]{1,0:T(1,128)} %refs_0_.3, f32[9,32,128]{2,1,0:T(8,128)} %bitcast.13, f32[9,32,128]{2,1,0:T(8,128)S(1)} %collective-permute-done.refs_2_, f32[9,32,128]{2,1,0:T(8,128)S(1)} %collective-permute-done.1.refs_3_, f32[9,32,128]{2,1,0:T(8,128)S(1)} %collective-permute-done.2.refs_4_), custom_call_target="tpu_custom_call" | custom-call | tf_op jit(solution)/shard_map/facet/pallas_call | solution.py:341
  15.6 5.5 %all-to-all-done = f32[32,1,512]{2,1,0:T(1,128)S(1)} async-done(((f32[32,1,512]{2,1,0:T(1,128)}), f32[32,1,512]{2,1,0:T(1,128)S(1)}, u32[]{:S(2)}, u32[]{:S(2)}) %all-to-all-start) | async-done | bytes 65568 | tf_op jit(solution)/shard_map/all_to_all | solution.py:336
  21.1 11.0 %wall.1 = (f32[32,128]{1,0:T(8,128)}, f32[3,16,128]{2,1,0:T(8,128)S(1)}, bf16[2048,128]{1,0:T(8,128)(2,1)S(1)}) custom-call(s32[1,2]{1,0:T(1,128)} %refs_0_.3, s32[1,2,32]{2,1,0:T(2,128)} %refs_1_.1, f32[2,15,32,128]{3,2,1,0:T(8,128)S(1)} %facet.1.refs_2_, f32[128,128]{1,0:T(8,128)S(1)} %bitcast.8), custom_call_target="tpu_custom_call" | custom-call | tf_op jit(solution)/shard_map/wall/pallas_call | solution.py:349
  32.1 2.5 %all-to-all-start.1 = ((f32[32,1,128]{2,1,0:T(1,128)}), f32[32,1,128]{2,1,0:T(1,128)S(1)}, u32[]{:S(2)}, u32[]{:S(2)}) async-start(f32[32,1,128]{2,1,0:T(1,128)} %bitcast.5), calls=%async_computation.1 | async-start | bytes 32768 | tf_op jit(solution)/shard_map/all_to_all | solution.py:366
  34.6 6.3 %pair.1 = f32[7,2048]{1,0:T(8,128)} custom-call(f32[128,128]{1,0:T(8,128)S(1)} %bitcast.9, f32[3,16,128]{2,1,0:T(8,128)S(1)} %get-tuple-element.5.force_ref, bf16[2048,128]{1,0:T(8,128)(2,1)S(1)} %get-tuple-element.6.left), custom_call_target="tpu_custom_call" | custom-call | tf_op jit(solution)/shard_map/pair/pallas_call | solution.py:369
  40.9 0.9 %all-to-all-done.1 = f32[32,1,128]{2,1,0:T(1,128)S(1)} async-done(((f32[32,1,128]{2,1,0:T(1,128)}), f32[32,1,128]{2,1,0:T(1,128)S(1)}, u32[]{:S(2)}, u32[]{:S(2)}) %all-to-all-start.1) | async-done | bytes 16416 | tf_op jit(solution)/shard_map/all_to_all | solution.py:366
  41.8 0.6 %slice_reduce_fusion = f32[6]{0:T(128)} fusion(f32[32,1,128]{2,1,0:T(1,128)S(1)} %all-to-all-done.1), kind=kLoop, calls=%fused_computation | loop fusion | flops 186 | bytes 792 | tf_op jit(solution)/shard_map/reduce_sum | solution.py:382
Async XLA Ops:
  0.6 13.1 %collective-permute-start.2 = (f32[9,32,128]{2,1,0:T(8,128)}, f32[9,32,128]{2,1,0:T(8,128)S(1)}, u32[]{:S(2)}, u32[]{:S(2)}) collective-permute-start(f32[9,32,128]{2,1,0:T(8,128)} %bitcast.10), channel_id=1, source_target_pairs={{0,24},{8,16},{16,8},{24,0},{1,25},{9,17},{17,9},{25,1},{2,26},{10... | collective-permute-start | bytes 442376 | tf_op jit(solution)/shard_map/ppermute | solution.py:333
  4.6 9.1 %collective-permute-start.1 = (f32[9,32,128]{2,1,0:T(8,128)}, f32[9,32,128]{2,1,0:T(8,128)S(1)}, u32[]{:S(2)}, u32[]{:S(2)}) collective-permute-start(f32[9,32,128]{2,1,0:T(8,128)} %bitcast.11), channel_id=1, source_target_pairs={{0,16},{8,24},{16,0},{24,8},{1,17},{9,25},{17,1},{25,9},{2,18},{10... | collective-permute-start | bytes 442376 | tf_op jit(solution)/shard_map/ppermute | solution.py:333
  5.1 8.6 %collective-permute-start = (f32[9,32,128]{2,1,0:T(8,128)}, f32[9,32,128]{2,1,0:T(8,128)S(1)}, u32[]{:S(2)}, u32[]{:S(2)}) collective-permute-start(f32[9,32,128]{2,1,0:T(8,128)} %bitcast.12), channel_id=1, source_target_pairs={{0,8},{8,0},{16,24},{24,16},{1,9},{9,1},{17,25},{25,17},{2,10},{10... | collective-permute-start | bytes 442376 | tf_op jit(solution)/shard_map/ppermute | solution.py:333
  7.4 13.6 %all-to-all-start = ((f32[32,1,512]{2,1,0:T(1,128)}), f32[32,1,512]{2,1,0:T(1,128)S(1)}, u32[]{:S(2)}, u32[]{:S(2)}) async-start(f32[32,1,512]{2,1,0:T(1,128)} %bitcast.1), calls=%async_computation | async-start | bytes 131072 | tf_op jit(solution)/shard_map/all_to_all | solution.py:336
  32.1 9.7 %all-to-all-start.1 = ((f32[32,1,128]{2,1,0:T(1,128)}), f32[32,1,128]{2,1,0:T(1,128)S(1)}, u32[]{:S(2)}, u32[]{:S(2)}) async-start(f32[32,1,128]{2,1,0:T(1,128)} %bitcast.5), calls=%async_computation.1 | async-start | bytes 32768 | tf_op jit(solution)/shard_map/all_to_all | solution.py:366
